TPU v7x, 32 devices: a whole 2x2x4 slice. The times are simulated.
32 devices in a mesh: seq: 8 (over z, x), head: 4 (over y, core).
Axes of the slice: x: 2, y: 2, z: 4, core: 2. Of those that a mesh axis runs over, the one named last changes fastest.
Arguments:
- tokens: bfloat16 [2, 2048, 2048], P(None, 'seq'), may hold values from -6 to 6
- w_query: bfloat16 [2048, 2048], P('seq', 'head'), may hold values from -0.125 to 0.125
- w_key: bfloat16 [2048, 2048], P('seq', 'head'), may hold values from -0.125 to 0.125
- w_value: bfloat16 [2048, 2048], P('seq', 'head'), may hold values from -0.125 to 0.125
- w_gate: bfloat16 [2048, 2048], P('seq', 'head'), may hold values from -0.125 to 0.125
- w_out: bfloat16 [2048, 2048], P('head', 'seq'), may hold values from -0.125 to 0.125
- w_first: bfloat16 [2048, 5632], P('seq', 'head'), may hold values from -0.125 to 0.125
- w_second: bfloat16 [2048, 5632], P('seq', 'head'), may hold values from -0.125 to 0.125
- w_down: bfloat16 [5632, 2048], P('head', 'seq'), may hold values from -0.078125 to 0.078125
- decay_rate: float32 [16], P('head'), may hold values from 7.6293945e-06 to 0.03125
- out_grad: bfloat16 [2, 2048, 2048], P(None, 'seq'), may hold values from -6 to 6
Outputs:
- layer_out: bfloat16 [2, 2048, 2048], P(None, 'seq')
- input_grad: float32 [2, 2048, 2048], P(None, 'seq')
- grad_query: float32 [2048, 2048], P('seq', 'head')
- grad_key: float32 [2048, 2048], P('seq', 'head')
- grad_value: float32 [2048, 2048], P('seq', 'head')
- grad_gate: float32 [2048, 2048], P('seq', 'head')
- grad_out: float32 [2048, 2048], P('head', 'seq')
- grad_first: float32 [2048, 5632], P('seq', 'head')
- grad_second: float32 [2048, 5632], P('seq', 'head')
- grad_down: float32 [5632, 2048], P('head', 'seq')
All inputs are finite; a program needn't handle non-finite values.
Results may differ from a plain program's by a relative error of at most 0.018.
Values may be sent and summed in bfloat16 or wider, within the bound.
No kernel may reach another device: no remote copies, remote signals or barrier semaphores. Data moves between devices by JAX's collectives and lax.ppermute only.
A program may use at most 256 MiB of HBM per device.

v0:
```python
import jax
import jax.numpy as jnp
from jax import lax
from jax.sharding import PartitionSpec as P

BLOCK = 256


EPSILON = 1e-06
HIGHEST = lax.Precision.HIGHEST


def entering(value, axis, join, neutral, backward):
    count, mine = (lax.axis_size(axis), lax.axis_index(axis))
    pieces = jax.tree.map(lambda part: lax.all_gather(part, axis), value)
    if backward:
        pieces = jax.tree.map(lambda part: part[::-1], pieces)
        mine = count - 1 - mine
    subtotal = jax.tree.map(
        lambda part, zero: jnp.full_like(part, 0) + jnp.asarray(zero, part.dtype), value, neutral
    )

    def hop(position, subtotal):
        longer = join(subtotal, jax.tree.map(lambda part: part[position], pieces))
        return jax.tree.map(lambda new, old: jnp.where(position < mine, new, old), longer, subtotal)

    return lax.fori_loop(0, count - 1, hop, subtotal)


def rms_scale(values):
    return lax.rsqrt(jnp.mean(values * values, axis=-1, keepdims=True) + EPSILON)


def rms_back(values, scale, upstream):
    feature_count = values.shape[-1]
    inner = jnp.sum(upstream * values, axis=-1, keepdims=True)
    return scale * upstream - scale * scale * scale / feature_count * values * inner


def silu_slope(values):
    sigma = jax.nn.sigmoid(values)
    return sigma * (1.0 + values * (1.0 - sigma))


def left_contract(left, right):
    return lax.dot_general(
        left, right, (((0,), (0,)), ((), ())), preferred_element_type=jnp.float32
    )


def right_contract(left, right):
    return lax.dot_general(
        left, right, (((1,), (1,)), ((), ())), preferred_element_type=jnp.float32
    )


def combine_states(earlier, later):
    return (earlier[0] * later[0], later[0][:, None, None] * earlier[1] + later[1])


def decay_tables(rates, row_count):
    positions = jnp.arange(row_count, dtype=jnp.float32)
    distance = positions[:, None] - positions[None, :]
    is_causal = distance >= 0
    decay_mask = jnp.where(
        is_causal[None],
        jnp.exp(-rates[:, None, None] * jnp.where(is_causal, distance, 0.0)[None]),
        0.0,
    )
    lead_decay = jnp.exp(-rates[None, :] * (positions[:, None] + 1.0))
    tail_decay = jnp.exp(-rates[None, :] * (row_count - 1.0 - positions[:, None]))
    block_decay = jnp.exp(-rates * row_count)
    return (decay_mask, lead_decay, tail_decay, block_decay)


def split_blocks(values, head_count, block_len):
    return values.reshape(values.shape[0] // block_len, block_len, head_count, -1)


def attend_forward(queries, keys_low, values_low, rates):
    row_count = queries.shape[0]
    head_count = rates.shape[0]
    block_len = BLOCK
    decay_mask, lead_decay, tail_decay, block_decay = decay_tables(rates, block_len)
    _, _, shard_tail, shard_decay = decay_tables(rates, row_count)
    key_flat = keys_low.reshape(row_count, head_count, -1).astype(jnp.float32)
    value_flat = values_low.reshape(row_count, head_count, -1).astype(jnp.float32)
    shard_state = jnp.einsum(
        "shd,she->hde", key_flat * shard_tail[:, :, None], value_flat, precision=HIGHEST
    )
    identity = (jnp.ones_like(shard_decay), jnp.zeros_like(shard_state))
    state_in = entering((shard_decay, shard_state), "seq", combine_states, identity, False)[1]

    def step(carry, pieces):
        query_heads, key_heads, value_heads = pieces
        scores = jnp.einsum(
            "thd,shd->hts", query_heads, key_heads, preferred_element_type=jnp.float32
        )
        weights = (scores * decay_mask).astype(jnp.bfloat16)
        intra = jnp.einsum("hts,shd->thd", weights, value_heads, preferred_element_type=jnp.float32)
        inter = jnp.einsum(
            "thd,hde->the",
            query_heads.astype(jnp.float32) * lead_decay[:, :, None],
            carry,
            precision=HIGHEST,
        )
        local_state = jnp.einsum(
            "shd,she->hde",
            key_heads.astype(jnp.float32) * tail_decay[:, :, None],
            value_heads.astype(jnp.float32),
            precision=HIGHEST,
        )
        new_state = block_decay[:, None, None] * carry + local_state
        return (new_state, (intra + inter, carry))

    pieces = (
        split_blocks(queries, head_count, block_len),
        split_blocks(keys_low, head_count, block_len),
        split_blocks(values_low, head_count, block_len),
    )
    _, (blocks_out, block_states) = lax.scan(step, state_in, pieces)
    return (blocks_out.reshape(row_count, -1), block_states)


def attend_backward(queries, keys_low, values_low, dattn, block_states, rates):
    row_count = queries.shape[0]
    head_count = rates.shape[0]
    block_len = BLOCK
    decay_mask, lead_decay, tail_decay, block_decay = decay_tables(rates, block_len)
    _, shard_lead, _, shard_decay = decay_tables(rates, row_count)
    query_flat = queries.reshape(row_count, head_count, -1).astype(jnp.float32)
    dattn_flat = dattn.reshape(row_count, head_count, -1).astype(jnp.float32)
    passed = jnp.einsum(
        "thd,the->hde", query_flat * shard_lead[:, :, None], dattn_flat, precision=HIGHEST
    )
    identity = (jnp.ones_like(shard_decay), jnp.zeros_like(passed))
    state_later = entering((shard_decay, passed), "seq", combine_states, identity, True)[1]

    def step(carry, pieces):
        query_heads, key_heads, value_heads, dattn_heads, state_in = pieces
        dattn_wide = dattn_heads.astype(jnp.float32)
        scores = jnp.einsum(
            "thd,shd->hts", query_heads, key_heads, preferred_element_type=jnp.float32
        )
        weights = (scores * decay_mask).astype(jnp.bfloat16)
        dweights = jnp.einsum(
            "the,she->hts", dattn_heads, value_heads, preferred_element_type=jnp.float32
        )
        dscores = (dweights * decay_mask).astype(jnp.bfloat16)
        dqueries = jnp.einsum(
            "hts,shd->thd", dscores, key_heads, preferred_element_type=jnp.float32
        )
        dqueries = dqueries + lead_decay[:, :, None] * jnp.einsum(
            "the,hde->thd", dattn_wide, state_in, precision=HIGHEST
        )
        dkeys = jnp.einsum("hts,thd->shd", dscores, query_heads, preferred_element_type=jnp.float32)
        dkeys = dkeys + tail_decay[:, :, None] * jnp.einsum(
            "she,hde->shd", value_heads.astype(jnp.float32), carry, precision=HIGHEST
        )
        dvalues = jnp.einsum(
            "hts,the->she", weights, dattn_heads, preferred_element_type=jnp.float32
        )
        dvalues = dvalues + tail_decay[:, :, None] * jnp.einsum(
            "shd,hde->she", key_heads.astype(jnp.float32), carry, precision=HIGHEST
        )
        local_pass = jnp.einsum(
            "thd,the->hde",
            query_heads.astype(jnp.float32) * lead_decay[:, :, None],
            dattn_wide,
            precision=HIGHEST,
        )
        new_carry = block_decay[:, None, None] * carry + local_pass
        return (new_carry, (dqueries, dkeys, dvalues))

    pieces = (
        split_blocks(queries, head_count, block_len),
        split_blocks(keys_low, head_count, block_len),
        split_blocks(values_low, head_count, block_len),
        split_blocks(dattn, head_count, block_len),
        block_states,
    )
    _, (dqueries, dkeys, dvalues) = lax.scan(step, state_later, pieces, reverse=True)
    return (
        dqueries.reshape(row_count, -1),
        dkeys.reshape(row_count, -1),
        dvalues.reshape(row_count, -1),
    )


def forward_pass(resid_in, gathered, rates):
    w_query, w_key, w_value, w_gate, w_out, w_first, w_second, w_down = gathered
    scale_in = rms_scale(resid_in)
    normed_in = (resid_in * scale_in).astype(jnp.bfloat16)
    query_pre = jnp.dot(normed_in, w_query, preferred_element_type=jnp.float32)
    key_pre = jnp.dot(normed_in, w_key, preferred_element_type=jnp.float32)
    queries = jax.nn.silu(query_pre).astype(jnp.bfloat16)
    keys_low = jax.nn.silu(key_pre).astype(jnp.bfloat16)
    values_low = jnp.dot(normed_in, w_value, preferred_element_type=jnp.float32).astype(
        jnp.bfloat16
    )
    gate_lin = jnp.dot(normed_in, w_gate, preferred_element_type=jnp.float32)
    attn_raw, block_states = attend_forward(queries, keys_low, values_low, rates)
    squares = lax.psum(jnp.sum(attn_raw * attn_raw, axis=1), "head")
    attn_scale = lax.rsqrt(squares[:, None] / resid_in.shape[-1] + EPSILON)
    attn_normed = attn_raw * attn_scale
    gated = (attn_normed * gate_lin).astype(jnp.bfloat16)
    resid_mid = resid_in + lax.psum(
        jnp.dot(gated, w_out, preferred_element_type=jnp.float32), "head"
    )
    scale_mid = rms_scale(resid_mid)
    normed_mid = (resid_mid * scale_mid).astype(jnp.bfloat16)
    first_pre = jnp.dot(normed_mid, w_first, preferred_element_type=jnp.float32)
    second_pre = jnp.dot(normed_mid, w_second, preferred_element_type=jnp.float32)
    product = (first_pre * second_pre).astype(jnp.bfloat16)
    result = resid_mid + lax.psum(
        jnp.dot(product, w_down, preferred_element_type=jnp.float32).astype(jnp.bfloat16), "head"
    ).astype(jnp.float32)
    kept = (
        resid_in,
        scale_in,
        normed_in,
        query_pre,
        key_pre,
        queries,
        keys_low,
        values_low,
        gate_lin,
        attn_raw,
        block_states,
        attn_scale,
        attn_normed,
        gated,
        resid_mid,
        scale_mid,
        normed_mid,
        first_pre,
        second_pre,
        product,
    )
    return (kept, result)


def backward_pass(upstream, kept, gathered, rates):
    w_query, w_key, w_value, w_gate, w_out, w_first, w_second, w_down = gathered
    (
        resid_in,
        scale_in,
        normed_in,
        query_pre,
        key_pre,
        queries,
        keys_low,
        values_low,
        gate_lin,
        attn_raw,
        block_states,
        attn_scale,
        attn_normed,
        gated,
        resid_mid,
        scale_mid,
        normed_mid,
        first_pre,
        second_pre,
        product,
    ) = kept
    grad_down = left_contract(product, upstream)
    dproduct = right_contract(upstream, w_down)
    dfirst = (dproduct * second_pre).astype(jnp.bfloat16)
    dsecond = (dproduct * first_pre).astype(jnp.bfloat16)
    grad_first = left_contract(normed_mid, dfirst)
    grad_second = left_contract(normed_mid, dsecond)
    dnormed_mid = lax.psum(
        right_contract(dfirst, w_first) + right_contract(dsecond, w_second), "head"
    )
    grad_mid = upstream.astype(jnp.float32) + rms_back(resid_mid, scale_mid, dnormed_mid)
    grad_mid_low = grad_mid.astype(jnp.bfloat16)
    grad_out = left_contract(gated, grad_mid_low)
    dgated = right_contract(grad_mid_low, w_out)
    dgate = (dgated * attn_normed).astype(jnp.bfloat16)
    dnormed = dgated * gate_lin
    inner = lax.psum(jnp.sum(dnormed * attn_raw, axis=1), "head")
    dattn = (
        attn_scale * dnormed
        - attn_scale * attn_scale * attn_scale / resid_in.shape[-1] * attn_raw * inner[:, None]
    )
    dqueries, dkeys, dvalues = attend_backward(
        queries, keys_low, values_low, dattn.astype(jnp.bfloat16), block_states, rates
    )
    dquery_pre = (dqueries * silu_slope(query_pre)).astype(jnp.bfloat16)
    dkey_pre = (dkeys * silu_slope(key_pre)).astype(jnp.bfloat16)
    dvalue_pre = dvalues.astype(jnp.bfloat16)
    grad_query = left_contract(normed_in, dquery_pre)
    grad_key = left_contract(normed_in, dkey_pre)
    grad_value = left_contract(normed_in, dvalue_pre)
    grad_gate = left_contract(normed_in, dgate)
    partial_in = (
        right_contract(dquery_pre, w_query)
        + right_contract(dkey_pre, w_key)
        + right_contract(dvalue_pre, w_value)
        + right_contract(dgate, w_gate)
    )
    dnormed_in = lax.psum(partial_in.astype(jnp.bfloat16), "head").astype(jnp.float32)
    input_grad = grad_mid + rms_back(resid_in, scale_in, dnormed_in)
    return (
        input_grad,
        (grad_query, grad_key, grad_value, grad_gate, grad_out, grad_first, grad_second, grad_down),
    )


def local(
    tokens, w_query, w_key, w_value, w_gate, w_out, w_first, w_second, w_down, decay_rate, out_grad
):
    micro_count = tokens.shape[0]
    outputs = []
    input_grads = []
    grad_total = None
    for which_batch in range(micro_count):
        gathered = (
            lax.all_gather(w_query, "seq", axis=0, tiled=True),
            lax.all_gather(w_key, "seq", axis=0, tiled=True),
            lax.all_gather(w_value, "seq", axis=0, tiled=True),
            lax.all_gather(w_gate, "seq", axis=0, tiled=True),
            lax.all_gather(w_out, "seq", axis=1, tiled=True),
            lax.all_gather(w_first, "seq", axis=0, tiled=True),
            lax.all_gather(w_second, "seq", axis=0, tiled=True),
            lax.all_gather(w_down, "seq", axis=1, tiled=True),
        )
        kept, result = forward_pass(tokens[which_batch].astype(jnp.float32), gathered, decay_rate)
        outputs.append(result.astype(jnp.bfloat16))
        gathered = (
            lax.all_gather(w_query, "seq", axis=0, tiled=True),
            lax.all_gather(w_key, "seq", axis=0, tiled=True),
            lax.all_gather(w_value, "seq", axis=0, tiled=True),
            lax.all_gather(w_gate, "seq", axis=0, tiled=True),
            lax.all_gather(w_out, "seq", axis=1, tiled=True),
            lax.all_gather(w_first, "seq", axis=0, tiled=True),
            lax.all_gather(w_second, "seq", axis=0, tiled=True),
            lax.all_gather(w_down, "seq", axis=1, tiled=True),
        )
        input_grad, grads = backward_pass(out_grad[which_batch], kept, gathered, decay_rate)
        input_grads.append(input_grad)
        grads = (
            lax.psum_scatter(
                grads[0].astype(jnp.bfloat16), "seq", scatter_dimension=0, tiled=True
            ).astype(jnp.float32),
            lax.psum_scatter(
                grads[1].astype(jnp.bfloat16), "seq", scatter_dimension=0, tiled=True
            ).astype(jnp.float32),
            lax.psum_scatter(
                grads[2].astype(jnp.bfloat16), "seq", scatter_dimension=0, tiled=True
            ).astype(jnp.float32),
            lax.psum_scatter(
                grads[3].astype(jnp.bfloat16), "seq", scatter_dimension=0, tiled=True
            ).astype(jnp.float32),
            lax.psum_scatter(
                grads[4].astype(jnp.bfloat16), "seq", scatter_dimension=1, tiled=True
            ).astype(jnp.float32),
            lax.psum_scatter(
                grads[5].astype(jnp.bfloat16), "seq", scatter_dimension=0, tiled=True
            ).astype(jnp.float32),
            lax.psum_scatter(
                grads[6].astype(jnp.bfloat16), "seq", scatter_dimension=0, tiled=True
            ).astype(jnp.float32),
            lax.psum_scatter(
                grads[7].astype(jnp.bfloat16), "seq", scatter_dimension=1, tiled=True
            ).astype(jnp.float32),
        )
        if grad_total is None:
            grad_total = tuple(grads)
        else:
            grad_total = tuple((total + grad for total, grad in zip(grad_total, grads)))
    return (
        jnp.stack(outputs),
        jnp.stack(input_grads),
        grad_total[0],
        grad_total[1],
        grad_total[2],
        grad_total[3],
        grad_total[4],
        grad_total[5],
        grad_total[6],
        grad_total[7],
    )


def solution(mesh):
    placed = (
        P(None, "seq", None),
        P("seq", "head"),
        P("seq", "head"),
        P("seq", "head"),
        P("seq", "head"),
        P("head", "seq"),
        P("seq", "head"),
        P("seq", "head"),
        P("head", "seq"),
        P("head"),
        P(None, "seq", None),
    )
    return jax.shard_map(
        local,
        mesh=mesh,
        in_specs=placed,
        out_specs=(
            P(None, "seq", None),
            P(None, "seq", None),
            P("seq", "head"),
            P("seq", "head"),
            P("seq", "head"),
            P("seq", "head"),
            P("head", "seq"),
            P("seq", "head"),
            P("seq", "head"),
            P("head", "seq"),
        ),
        check_vma=False,
    )
```

profile of v0, /device:TPU:0, one launch (start us, length us, event | category | flops | bytes accessed | tf_op | source)
XLA Modules:
  0.0 2507.8 jit_solution(15061958254171162375)
XLA Ops:
  14.2 47.9 %all-gather.22.cloned.1.call-done = bf16[2048,512]{1,0:T(8,128)(2,1)} async-done(((bf16[256,512]{1,0:T(8,128)(2,1)}), bf16[2048,512]{1,0:T(8,128)(2,1)}) %all-gather.22.cloned.1.call-update) | async-done | bytes 2097168 | tf_op jit(solution)/shard_map/all_gather | solution.py:321
  65.9 46.2 %all-gather.18.cloned.1.call-done = bf16[2048,512]{1,0:T(8,128)(2,1)} async-done(((bf16[256,512]{1,0:T(8,128)(2,1)}), bf16[2048,512]{1,0:T(8,128)(2,1)}) %all-gather.18.cloned.1.call-update) | async-done | bytes 2097168 | tf_op jit(solution)/shard_map/all_gather | solution.py:322
  117.0 18.9 all-reduce
  136.0 26.3 %all-gather.20.cloned.1.call-done = bf16[2048,512]{1,0:T(8,128)(2,1)} async-done(((bf16[256,512]{1,0:T(8,128)(2,1)}), bf16[2048,512]{1,0:T(8,128)(2,1)}) %all-gather.20.cloned.1.call-update) | async-done | bytes 2097168 | tf_op jit(solution)/shard_map/all_gather | solution.py:320
  168.2 44.5 %all-gather.34.cloned.1.call-done = f32[32,128,128]{2,1,0:T(8,128)} async-done(((f32[4,128,128]{2,1,0:T(8,128)}), f32[32,128,128]{2,1,0:T(8,128)}) %all-gather.34.cloned.1.call-update) | async-done | bytes 2097168 | tf_op jit(solution)/shard_map/all_gather | solution.py:15
  212.7 7.6 while.36
  223.1 6.1 psum.84
  229.1 33.3 %all-gather.24.cloned.1.call-done = bf16[2048,512]{1,0:T(8,128)(2,1)} async-done(((bf16[256,512]{1,0:T(8,128)(2,1)}), bf16[2048,512]{1,0:T(8,128)(2,1)}) %all-gather.24.cloned.1.call-update) | async-done | bytes 2097168 | tf_op jit(solution)/shard_map/all_gather | solution.py:323
  265.6 48.4 %all-gather.26.cloned.1.call-done = bf16[512,2048]{1,0:T(8,128)(2,1)} async-done(((bf16[512,256]{1,0:T(8,128)(2,1)}), bf16[512,2048]{1,0:T(8,128)(2,1)}) %all-gather.26.cloned.1.call-update) | async-done | bytes 2097168 | tf_op jit(solution)/shard_map/all_gather | solution.py:324
  319.7 47.6 %all-reduce.9.cloned.1.call-done = f32[256,2048]{1,0:T(8,128)} async-done(((f32[256,2048]{1,0:T(8,128)}), f32[256,2048]{1,0:T(8,128)}) %all-reduce.9.cloned.1.call-update) | async-done | bytes 2097168 | tf_op jit(solution)/shard_map/psum | solution.py:207
  385.5 77.8 %all-gather.32.cloned.1.call-done = bf16[1408,2048]{1,0:T(8,128)(2,1)} async-done(((bf16[1408,256]{1,0:T(8,128)(2,1)}), bf16[1408,2048]{1,0:T(8,128)(2,1)}) %all-gather.32.cloned.1.call-update) | async-done | bytes 5767184 | tf_op jit(solution)/shard_map/all_gather | solution.py:327
  463.3 5.9 fusion.62
  469.2 87.4 %all-gather.30.cloned.1.call-done = bf16[2048,1408]{1,0:T(8,128)(2,1)} async-done(((bf16[256,1408]{1,0:T(8,128)(2,1)}), bf16[2048,1408]{1,0:T(8,128)(2,1)}) %all-gather.30.cloned.1.call-update) | async-done | bytes 5767184 | tf_op jit(solution)/shard_map/all_gather | solution.py:326
  556.6 5.5 fusion.149
  562.1 87.6 %all-gather.28.cloned.1.call-done = bf16[2048,1408]{1,0:T(8,128)(2,1)} async-done(((bf16[256,1408]{1,0:T(8,128)(2,1)}), bf16[2048,1408]{1,0:T(8,128)(2,1)}) %all-gather.28.cloned.1.call-update) | async-done | bytes 5767184 | tf_op jit(solution)/shard_map/all_gather | solution.py:325
  649.7 6.3 multiply_convert_fusion.7
  662.4 37.7 %all-gather.36.cloned.1.call-done = f32[32,128,128]{2,1,0:T(8,128)} async-done(((f32[4,128,128]{2,1,0:T(8,128)}), f32[32,128,128]{2,1,0:T(8,128)}) %all-gather.36.cloned.1.call-update) | async-done | bytes 2097168 | tf_op jit(solution)/shard_map/all_gather | solution.py:15
  700.1 7.6 while.37
  710.4 5.6 psum.87
  724.7 84.1 %all-reduce.15.cloned.1.call-done = (f32[256,2048]{1,0:T(8,128)}, f32[256,2048]{1,0:T(8,128)}) async-done(((f32[256,2048]{1,0:T(8,128)}, f32[256,2048]{1,0:T(8,128)}), (f32[256,2048]{1,0:T(8,128)}, f32[256,2048]{1,0:T(8,128)})) %all-reduce.15.cloned.1.call-update) | async-done | bytes 4194320 | tf_op jit(solution)/shard_map/psum | solution.py:273
  817.7 5.8 psum.91
  861.9 20.2 all-gather.38.cloned.1.call-done
  885.4 7.7 while.38
  906.0 28.3 %all-reduce.13.cloned.1.call-done = f32[256,2048]{1,0:T(8,128)} async-done(((f32[256,2048]{1,0:T(8,128)}), f32[256,2048]{1,0:T(8,128)}) %all-reduce.13.cloned.1.call-update) | async-done | bytes 2097168 | tf_op jit(solution)/shard_map/psum | solution.py:273
  934.3 39.1 %all-reduce.11.cloned.1.call-done = bf16[256,2048]{1,0:T(8,128)(2,1)} async-done(((bf16[256,2048]{1,0:T(8,128)(2,1)}), bf16[256,2048]{1,0:T(8,128)(2,1)}) %all-reduce.11.cloned.1.call-update) | async-done | bytes 1048592 | tf_op jit(solution)/shard_map/psum | solution.py:303
  981.6 6.0 psum.94
  1017.5 5.7 convolution_convert_fusion.17
  1023.2 5.6 convolution_convert_fusion.16
  1036.9 6.7 all-gather.40.cloned.1.call-done
  1046.8 7.7 while.39
  1073.6 5.7 convolution_convert_fusion.2
  1092.8 5.5 convolution_convert_fusion.1
  1115.3 68.8 %reduce-scatter.35.cloned.1.call-done = bf16[512,256]{1,0:T(8,128)(2,1)} async-done(((bf16[512,2048]{1,0:T(8,128)(2,1)}), bf16[512,256]{1,0:T(8,128)(2,1)}) %reduce-scatter.35.cloned.1.call-update) | async-done | bytes 262160 | tf_op jit(solution)/shard_map/reduce_scatter | solution.py:356
  1186.0 68.2 %reduce-scatter.17.cloned.1.call-done = bf16[256,512]{1,0:T(8,128)(2,1)} async-done(((bf16[2048,512]{1,0:T(8,128)(2,1)}), bf16[256,512]{1,0:T(8,128)(2,1)}) %reduce-scatter.17.cloned.1.call-update) | async-done | bytes 262160 | tf_op jit(solution)/shard_map/reduce_scatter | solution.py:344
  1254.3 69.9 %reduce-scatter.19.cloned.1.call-done = bf16[256,512]{1,0:T(8,128)(2,1)} async-done(((bf16[2048,512]{1,0:T(8,128)(2,1)}), bf16[256,512]{1,0:T(8,128)(2,1)}) %reduce-scatter.19.cloned.1.call-update) | async-done | bytes 262160 | tf_op jit(solution)/shard_map/reduce_scatter | solution.py:344
  1326.1 68.3 %reduce-scatter.29.cloned.1.call-done = bf16[256,512]{1,0:T(8,128)(2,1)} async-done(((bf16[2048,512]{1,0:T(8,128)(2,1)}), bf16[256,512]{1,0:T(8,128)(2,1)}) %reduce-scatter.29.cloned.1.call-update) | async-done | bytes 262160 | tf_op jit(solution)/shard_map/reduce_scatter | solution.py:353
  1394.3 70.1 %reduce-scatter.31.cloned.1.call-done = bf16[256,512]{1,0:T(8,128)(2,1)} async-done(((bf16[2048,512]{1,0:T(8,128)(2,1)}), bf16[256,512]{1,0:T(8,128)(2,1)}) %reduce-scatter.31.cloned.1.call-update) | async-done | bytes 262160 | tf_op jit(solution)/shard_map/reduce_scatter | solution.py:353
  1466.3 69.7 %all-reduce.17.cloned.1.call-done = (bf16[256,2048]{1,0:T(8,128)(2,1)}, bf16[256,2048]{1,0:T(8,128)(2,1)}, bf16[256,2048]{1,0:T(8,128)(2,1)}) async-done(((bf16[256,2048]{1,0:T(8,128)(2,1)}, bf16[256,2048]{1,0:T(8,128)(2,1)}, bf16[256,2048]{1,0:T(8,128)(2,1)}), (bf16[256,2048]{1,0:T(8,128)(2,1)}, bf16[256,2048]{1,0:T(8,128)(2,1)}, bf16[256,2048]{1,0:T(8,128)(2,1)})) %all-reduce.17.cloned.1.call-update) | async-done | bytes 3145744 | tf_op jit(solution)/shard_map/psum | solution.py:215
  1546.1 103.5 %reduce-scatter.41.cloned.1.call-done = bf16[256,1408]{1,0:T(8,128)(2,1)} async-done(((bf16[2048,1408]{1,0:T(8,128)(2,1)}), bf16[256,1408]{1,0:T(8,128)(2,1)}) %reduce-scatter.41.cloned.1.call-update) | async-done | bytes 720912 | tf_op jit(solution)/shard_map/reduce_scatter | solution.py:362
  1649.6 113.4 %reduce-scatter.43.cloned.1.call-done = bf16[256,1408]{1,0:T(8,128)(2,1)} async-done(((bf16[2048,1408]{1,0:T(8,128)(2,1)}), bf16[256,1408]{1,0:T(8,128)(2,1)}) %reduce-scatter.43.cloned.1.call-update) | async-done | bytes 720912 | tf_op jit(solution)/shard_map/reduce_scatter | solution.py:362
  1765.6 110.8 %reduce-scatter.37.cloned.1.call-done = bf16[256,1408]{1,0:T(8,128)(2,1)} async-done(((bf16[2048,1408]{1,0:T(8,128)(2,1)}), bf16[256,1408]{1,0:T(8,128)(2,1)}) %reduce-scatter.37.cloned.1.call-update) | async-done | bytes 720912 | tf_op jit(solution)/shard_map/reduce_scatter | solution.py:359
  1876.3 113.3 %reduce-scatter.39.cloned.1.call-done = bf16[256,1408]{1,0:T(8,128)(2,1)} async-done(((bf16[2048,1408]{1,0:T(8,128)(2,1)}), bf16[256,1408]{1,0:T(8,128)(2,1)}) %reduce-scatter.39.cloned.1.call-update) | async-done | bytes 720912 | tf_op jit(solution)/shard_map/reduce_scatter | solution.py:359
  1992.2 111.3 %reduce-scatter.45.cloned.1.call-done = bf16[1408,256]{1,0:T(8,128)(2,1)} async-done(((bf16[1408,2048]{1,0:T(8,128)(2,1)}), bf16[1408,256]{1,0:T(8,128)(2,1)}) %reduce-scatter.45.cloned.1.call-update) | async-done | bytes 720912 | tf_op jit(solution)/shard_map/reduce_scatter | solution.py:365
  2103.5 113.8 %reduce-scatter.47.cloned.1.call-done = bf16[1408,256]{1,0:T(8,128)(2,1)} async-done(((bf16[1408,2048]{1,0:T(8,128)(2,1)}), bf16[1408,256]{1,0:T(8,128)(2,1)}) %reduce-scatter.47.cloned.1.call-update) | async-done | bytes 720912 | tf_op jit(solution)/shard_map/reduce_scatter | solution.py:365
  2219.9 68.3 %reduce-scatter.21.cloned.1.call-done = bf16[256,512]{1,0:T(8,128)(2,1)} async-done(((bf16[2048,512]{1,0:T(8,128)(2,1)}), bf16[256,512]{1,0:T(8,128)(2,1)}) %reduce-scatter.21.cloned.1.call-update) | async-done | bytes 262160 | tf_op jit(solution)/shard_map/reduce_scatter | solution.py:347
  2288.1 70.2 %reduce-scatter.23.cloned.1.call-done = bf16[256,512]{1,0:T(8,128)(2,1)} async-done(((bf16[2048,512]{1,0:T(8,128)(2,1)}), bf16[256,512]{1,0:T(8,128)(2,1)}) %reduce-scatter.23.cloned.1.call-update) | async-done | bytes 262160 | tf_op jit(solution)/shard_map/reduce_scatter | solution.py:347
  2360.2 68.3 %reduce-scatter.25.cloned.1.call-done = bf16[256,512]{1,0:T(8,128)(2,1)} async-done(((bf16[2048,512]{1,0:T(8,128)(2,1)}), bf16[256,512]{1,0:T(8,128)(2,1)}) %reduce-scatter.25.cloned.1.call-update) | async-done | bytes 262160 | tf_op jit(solution)/shard_map/reduce_scatter | solution.py:350
  2428.5 70.0 %reduce-scatter.27.cloned.1.call-done = bf16[256,512]{1,0:T(8,128)(2,1)} async-done(((bf16[2048,512]{1,0:T(8,128)(2,1)}), bf16[256,512]{1,0:T(8,128)(2,1)}) %reduce-scatter.27.cloned.1.call-update) | async-done | bytes 262160 | tf_op jit(solution)/shard_map/reduce_scatter | solution.py:350
  (427 shorter events, 286.8 us)
Async XLA Ops:
  7.2 55.0 %all-gather.22.cloned.1.call-start = ((), (), s32[]{:S(2)}) async-start(), calls=%async_computation.18 | async-start | bytes 2359296 | tf_op jit(solution)/shard_map/all_gather | solution.py:321
  7.9 104.2 %all-gather.18.cloned.1.call-start = ((), (), s32[]{:S(2)}) async-start(), calls=%async_computation.16 | async-start | bytes 2359296 | tf_op jit(solution)/shard_map/all_gather | solution.py:322
  8.7 153.7 %all-gather.20.cloned.1.call-start = ((), (), s32[]{:S(2)}) async-start(), calls=%async_computation.17 | async-start | bytes 2359296 | tf_op jit(solution)/shard_map/all_gather | solution.py:320
  9.4 203.3 %all-gather.34.cloned.1.call-start = ((), (), s32[]{:S(2)}) async-start(), calls=%async_computation.43 | async-start | bytes 2359296 | tf_op jit(solution)/shard_map/all_gather | solution.py:15
  62.2 49.9 %copy-start = (bf16[2,256,2048]{2,1,0:T(8,128)(2,1)S(1)}, bf16[2,256,2048]{2,1,0:T(8,128)(2,1)}, u32[]{:S(2)}) copy-start(bf16[2,256,2048]{2,1,0:T(8,128)(2,1)} %param.19) | copy-start | bytes 6291460
  65.8 100.9 %copy-start.69 = (bf16[256,512]{1,0:T(8,128)(2,1)}, bf16[256,512]{1,0:T(8,128)(2,1)S(1)}, u32[]{:S(2)}) copy-start(bf16[256,512]{1,0:T(8,128)(2,1)S(1)} %get-tuple-element.697) | copy-start | bytes 786436
  65.9 48.5 %copy-start.47 = (bf16[256,512]{0,1:T(8,128)(2,1)}, bf16[256,512]{0,1:T(8,128)(2,1)S(1)}, u32[]{:S(2)}) copy-start(bf16[256,512]{0,1:T(8,128)(2,1)S(1)} %copy.226) | copy-start | bytes 786436
  114.4 52.7 %copy-start.49 = (bf16[32,4,8,128]{3,2,1,0:T(8,128)(2,1)}, bf16[32,4,8,128]{3,2,1,0:T(8,128)(2,1)S(1)}, u32[]{:S(2)}) copy-start(bf16[32,4,8,128]{3,2,1,0:T(8,128)(2,1)S(1)} %fusion.50) | copy-start | bytes 786436
  115.6 146.9 %all-gather.24.cloned.1.call-start = ((), (), s32[]{:S(2)}) async-start(), calls=%async_computation.19 | async-start | bytes 2359296 | tf_op jit(solution)/shard_map/all_gather | solution.py:323
  116.2 197.8 %all-gather.26.cloned.1.call-start = ((), (), s32[]{:S(2)}) async-start(), calls=%async_computation.20 | async-start | bytes 2359296 | tf_op jit(solution)/shard_map/all_gather | solution.py:324
  116.7 250.6 %all-reduce.9.cloned.1.call-start = ((), (), s32[]{:S(2)}) async-start(), calls=%async_computation.21 | async-start | bytes 4194304 | tf_op jit(solution)/shard_map/psum | solution.py:207
  116.9 49.7 %copy-start.78 = (f32[256,256]{1,0:T(8,128)}, f32[256,256]{1,0:T(8,128)S(1)}, u32[]{:S(2)}) copy-start(f32[256,256]{1,0:T(8,128)S(1)} %fusion.108) | copy-start | bytes 786436
  166.6 53.7 %copy-start.35 = (bf16[256,512]{0,1:T(8,128)(2,1)}, bf16[256,512]{0,1:T(8,128)(2,1)S(1)}, u32[]{:S(2)}) copy-start(bf16[256,512]{0,1:T(8,128)(2,1)S(1)} %copy.169) | copy-start | bytes 786436
  220.3 45.3 %copy-start.17 = (f32[4,128,128]{2,1,0:T(8,128)}, f32[4,128,128]{2,1,0:T(8,128)S(1)}, u32[]{:S(2)}) copy-start(f32[4,128,128]{2,1,0:T(8,128)S(1)} %get-tuple-element.536) | copy-start | bytes 786436
  223.0 42.6 %copy-start.27 = (f32[256,512]{1,0:T(8,128)}, f32[256,512]{1,0:T(8,128)S(1)}, u32[]{:S(2)}) copy-start(f32[256,512]{1,0:T(8,128)S(1)} %copy.121) | copy-start | bytes 1572868
  265.6 52.0 %copy-start.59 = (bf16[256,512]{1,0:T(8,128)(2,1)}, bf16[256,512]{1,0:T(8,128)(2,1)S(1)}, u32[]{:S(2)}) copy-start(bf16[256,512]{1,0:T(8,128)(2,1)S(1)} %get-tuple-element.701) | copy-start | bytes 786436
  317.6 145.7 %all-gather.32.cloned.1.call-start = ((), (), s32[]{:S(2)}) async-start(), calls=%async_computation.24 | async-start | bytes 6488064 | tf_op jit(solution)/shard_map/all_gather | solution.py:327
  318.4 238.2 %all-gather.30.cloned.1.call-start = ((), (), s32[]{:S(2)}) async-start(), calls=%async_computation.23 | async-start | bytes 6488064 | tf_op jit(solution)/shard_map/all_gather | solution.py:326
  319.1 330.6 %all-gather.28.cloned.1.call-start = ((), (), s32[]{:S(2)}) async-start(), calls=%async_computation.22 | async-start | bytes 6488064 | tf_op jit(solution)/shard_map/all_gather | solution.py:325
  319.7 380.4 %all-gather.36.cloned.1.call-start = ((), (), s32[]{:S(2)}) async-start(), calls=%async_computation.44 | async-start | bytes 2359296 | tf_op jit(solution)/shard_map/all_gather | solution.py:15
  371.9 7.1 copy-start.32
  381.2 427.7 %all-reduce.15.cloned.1.call-start = ((), (), s32[]{:S(2)}) async-start(), calls=%async_computation.47 | async-start | bytes 8388608 | tf_op jit(solution)/shard_map/psum | solution.py:273
  707.8 13.7 copy-start.15
  724.3 157.9 %all-gather.38.cloned.1.call-start = ((), (), s32[]{:S(2)}) async-start(), calls=%async_computation.45 | async-start | bytes 2359296 | tf_op jit(solution)/shard_map/all_gather | solution.py:15
  832.1 102.2 %all-reduce.13.cloned.1.call-start = ((), (), s32[]{:S(2)}) async-start(), calls=%async_computation.26 | async-start | bytes 4194304 | tf_op jit(solution)/shard_map/psum | solution.py:273
  843.2 6.8 slice-start
  857.9 115.5 %all-reduce.11.cloned.1.call-start = ((), (), s32[]{:S(2)}) async-start(), calls=%async_computation.25 | async-start | bytes 2097152 | tf_op jit(solution)/shard_map/psum | solution.py:303
  906.0 137.7 %all-gather.40.cloned.1.call-start = ((), (), s32[]{:S(2)}) async-start(), calls=%async_computation.46 | async-start | bytes 2359296 | tf_op jit(solution)/shard_map/all_gather | solution.py:15
  981.6 10.2 copy-start.33
  993.8 121.5 %reduce-scatter.33.cloned.1.call-start = ((), (), s32[]{:S(2)}) async-start(), calls=%async_computation.35 | async-start | bytes 2359296 | tf_op jit(solution)/shard_map/reduce_scatter | solution.py:356
  997.7 186.5 %reduce-scatter.35.cloned.1.call-start = ((), (), s32[]{:S(2)}) async-start(), calls=%async_computation.36 | async-start | bytes 2359296 | tf_op jit(solution)/shard_map/reduce_scatter | solution.py:356
  1002.3 251.9 %reduce-scatter.17.cloned.1.call-start = ((), (), s32[]{:S(2)}) async-start(), calls=%async_computation.27 | async-start | bytes 2359296 | tf_op jit(solution)/shard_map/reduce_scatter | solution.py:344
  1005.5 318.7 %reduce-scatter.19.cloned.1.call-start = ((), (), s32[]{:S(2)}) async-start(), calls=%async_computation.28 | async-start | bytes 2359296 | tf_op jit(solution)/shard_map/reduce_scatter | solution.py:344
  1015.0 379.3 %reduce-scatter.29.cloned.1.call-start = ((), (), s32[]{:S(2)}) async-start(), calls=%async_computation.33 | async-start | bytes 2359296 | tf_op jit(solution)/shard_map/reduce_scatter | solution.py:353
  1017.2 447.2 %reduce-scatter.31.cloned.1.call-start = ((), (), s32[]{:S(2)}) async-start(), calls=%async_computation.34 | async-start | bytes 2359296 | tf_op jit(solution)/shard_map/reduce_scatter | solution.py:353
  1033.1 502.8 %all-reduce.17.cloned.1.call-start = ((), (), s32[]{:S(2)}) async-start(), calls=%async_computation.48 | async-start | bytes 6291456 | tf_op jit(solution)/shard_map/psum | solution.py:215
  1068.0 581.5 %reduce-scatter.41.cloned.1.call-start = ((), (), s32[]{:S(2)}) async-start(), calls=%async_computation.39 | async-start | bytes 6488064 | tf_op jit(solution)/shard_map/reduce_scatter | solution.py:362
  1073.5 689.5 %reduce-scatter.43.cloned.1.call-start = ((), (), s32[]{:S(2)}) async-start(), calls=%async_computation.40 | async-start | bytes 6488064 | tf_op jit(solution)/shard_map/reduce_scatter | solution.py:362
  1079.3 797.0 %reduce-scatter.37.cloned.1.call-start = ((), (), s32[]{:S(2)}) async-start(), calls=%async_computation.37 | async-start | bytes 6488064 | tf_op jit(solution)/shard_map/reduce_scatter | solution.py:359
  1085.1 904.5 %reduce-scatter.39.cloned.1.call-start = ((), (), s32[]{:S(2)}) async-start(), calls=%async_computation.38 | async-start | bytes 6488064 | tf_op jit(solution)/shard_map/reduce_scatter | solution.py:359
  1091.7 1011.8 %reduce-scatter.45.cloned.1.call-start = ((), (), s32[]{:S(2)}) async-start(), calls=%async_computation.41 | async-start | bytes 6488064 | tf_op jit(solution)/shard_map/reduce_scatter | solution.py:365
  1098.3 1118.9 %reduce-scatter.47.cloned.1.call-start = ((), (), s32[]{:S(2)}) async-start(), calls=%async_computation.42 | async-start | bytes 6488064 | tf_op jit(solution)/shard_map/reduce_scatter | solution.py:365
  1105.0 1183.2 %reduce-scatter.21.cloned.1.call-start = ((), (), s32[]{:S(2)}) async-start(), calls=%async_computation.29 | async-start | bytes 2359296 | tf_op jit(solution)/shard_map/reduce_scatter | solution.py:347
  1108.1 1250.2 %reduce-scatter.23.cloned.1.call-start = ((), (), s32[]{:S(2)}) async-start(), calls=%async_computation.30 | async-start | bytes 2359296 | tf_op jit(solution)/shard_map/reduce_scatter | solution.py:347
  1110.4 1318.1 %reduce-scatter.25.cloned.1.call-start = ((), (), s32[]{:S(2)}) async-start(), calls=%async_computation.31 | async-start | bytes 2359296 | tf_op jit(solution)/shard_map/reduce_scatter | solution.py:350
  1112.7 1385.8 %reduce-scatter.27.cloned.1.call-start = ((), (), s32[]{:S(2)}) async-start(), calls=%async_computation.32 | async-start | bytes 2359296 | tf_op jit(solution)/shard_map/reduce_scatter | solution.py:350
  1115.3 420.7 %copy-start.38 = (bf16[256,2048]{1,0:T(8,128)(2,1)S(1)}, bf16[256,2048]{1,0:T(8,128)(2,1)}, u32[]{:S(2)}) copy-start(bf16[256,2048]{1,0:T(8,128)(2,1)} %all-reduce.11.cloned.1.call-done) | copy-start | bytes 3145732
  1115.3 420.7 %copy-start.79 = (f32[256]{0:T(256)S(1)}, f32[256]{0:T(256)}, u32[]{:S(2)}) copy-start(f32[256]{0:T(256)} %get-tuple-element.679) | copy-start | bytes 3076
  (74 other events, 220.9 us)
Sparse Core Ops, SparseCore 0:
  10.1 51.9 all-gather.21
  64.3 47.7 all-gather.17
  114.2 48.0 all-gather.19
  164.9 47.7 all-gather.33
  214.7 47.7 all-gather.23
  264.4 49.5 all-gather.25
  317.7 49.5 all-reduce.8
  369.6 93.6 all-gather.31
  465.7 90.8 all-gather.29
  558.8 90.8 all-gather.27
  652.6 47.4 all-gather.35
  724.4 84.4 all-reduce.14
  832.2 49.8 all-gather.37
  884.4 49.8 all-reduce.12
  937.2 36.1 all-reduce.10
  994.0 49.6 all-gather.39
  1047.0 66.5 reduce-scatter.32
  1117.0 67.0 reduce-scatter.34
  1187.7 66.5 reduce-scatter.16
  1257.6 66.4 reduce-scatter.18
  1327.7 66.5 reduce-scatter.28
  1397.9 66.5 reduce-scatter.30
  1468.1 67.8 all-reduce.16
  1539.5 110.0 reduce-scatter.40
  1653.2 109.7 reduce-scatter.42
  1766.5 109.7 reduce-scatter.36
  1879.8 109.7 reduce-scatter.38
  1993.3 110.1 reduce-scatter.44
  2107.2 110.0 reduce-scatter.46
  2220.7 67.4 reduce-scatter.20
  2291.7 66.5 reduce-scatter.22
  2361.8 66.5 reduce-scatter.24
  2431.9 66.5 reduce-scatter.26
where the time goes:
time: 2520 us; the launch traced here: 2510 us
  waiting for transfers between devices  2130 us (85%)
  matrix products  194 us (8%)
  other arithmetic  83.1 us (3%)
  blocking collectives  42.4 us (2%)
  local copies, waits for them, and re-layouts  41.7 us (2%)
    reduce_scatter x2, waiting for transfers between devices, local(): lax.psum_scatter(grads[7].astype(jnp.bfloat16), 'seq', scatter_dimension=...  225 us
    reduce_scatter x2, waiting for transfers between devices, local(): lax.psum_scatter(grads[5].astype(jnp.bfloat16), 'seq', scatter_dimension=...  224 us
    reduce_scatter x2, waiting for transfers between devices, local(): lax.psum_scatter(grads[6].astype(jnp.bfloat16), 'seq', scatter_dimension=...  217 us
    reduce_scatter x2, waiting for transfers between devices, local(): lax.psum_scatter(grads[1].astype(jnp.bfloat16), 'seq', scatter_dimension=...  138 us
    reduce_scatter x2, waiting for transfers between devices, local(): lax.psum_scatter(grads[3].astype(jnp.bfloat16), 'seq', scatter_dimension=...  138 us
    reduce_scatter x2, waiting for transfers between devices, local(): lax.psum_scatter(grads[2].astype(jnp.bfloat16), 'seq', scatter_dimension=...  138 us
    reduce_scatter x2, waiting for transfers between devices, local(): lax.psum_scatter(grads[0].astype(jnp.bfloat16), 'seq', scatter_dimension=...  138 us
    psum x2, waiting for transfers between devices, backward_pass(): lax.psum(right_contract(dfirst, w_first) + right_contract(dsecond, w_seco...  112 us
  transfers between devices with their start and end apart: 33, of which 32 were waited for; matrix products, arithmetic and copies ran while one was open for 10% of the time, Pallas kernels for 0%

commit v1 on v0

v1 whole, which is shorter than its diff:
```python
import jax
import jax.numpy as jnp
from jax import lax
from jax.sharding import Mesh
from jax.sharding import PartitionSpec as P

EPSILON = 1e-06
BF16 = jnp.bfloat16
F32 = jnp.float32
PLANE = 2
SWAP = [(0, 1), (1, 0)]


def dot_nn(left, right):
    return jnp.dot(left, right, preferred_element_type=F32)


def dot_tn(left, right):
    return lax.dot_general(left, right, (((0,), (0,)), ((), ())), preferred_element_type=F32)


def dot_nt(left, right):
    return lax.dot_general(left, right, (((1,), (1,)), ((), ())), preferred_element_type=F32)


def after(value, *earlier):
    return lax.optimization_barrier((value, earlier))[0]


def swap_u(value):
    return lax.ppermute(value, "u", SWAP)


def swap_h(value, bit):
    count = lax.axis_size("head")
    return lax.ppermute(value, "head", [(i, i ^ bit) for i in range(count)])


def shift_t(value, by):
    count = lax.axis_size("t")
    return lax.ppermute(
        value, "t", [(i, i + by) for i in range(count) if 0 <= i + by < count]
    )


def is_line():
    return lax.axis_size("t") <= 4


def shift_of():
    return lax.axis_index("t") if is_line() else jnp.int32(0)


def rotate(values, back=False):
    count = lax.axis_size("t")
    if not is_line():
        return values
    width = values.shape[-1] // count
    start = shift_of()
    start = (count - start) if back else start
    blocks = [
        lax.dynamic_slice_in_dim(
            values, ((start + r) % count) * width, width, axis=values.ndim - 1
        )
        for r in range(count)
    ]
    return jnp.concatenate(blocks, axis=-1)


def gather_t(pieces):
    count = lax.axis_size("t")
    if not is_line():
        whole = lax.all_gather(pieces, "t")
        return [whole[r] for r in range(count)], pieces
    mine = lax.axis_index("t")
    up, down = pieces, pieces
    ups, downs = [], []
    for step in range(1, count):
        up = lax.ppermute(up, "t", [(i, i + 1) for i in range(step - 1, count - 1)])
        down = lax.ppermute(down, "t", [(i + 1, i) for i in range(0, count - step)])
        ups.append(up)
        downs.append(down)
    slots = [pieces]
    for r in range(1, count):
        slots.append(jnp.where(mine + r < count, downs[r - 1], ups[count - r - 1]))
    return slots, (up, down)


def scatter_t(slots):
    count = lax.axis_size("t")
    if not is_line():
        whole = jnp.stack([slot.astype(BF16) for slot in slots])
        return lax.psum_scatter(whole, "t", scatter_dimension=0, tiled=False).astype(F32)
    up = slots[count - 1].astype(BF16)
    down = slots[1].astype(BF16)
    for step in range(count - 1, 0, -1):
        up = lax.ppermute(up, "t", [(i, i + 1) for i in range(0, count - step)])
        down = lax.ppermute(down, "t", [(i + 1, i) for i in range(step - 1, count - 1)])
        if step > 1:
            up = (up.astype(F32) + slots[step - 1]).astype(BF16)
            down = (down.astype(F32) + slots[count - step + 1]).astype(BF16)
    return slots[0].astype(F32) + up.astype(F32) + down.astype(F32)


def plane_reduce(partial):
    rows, width = partial.shape
    parts = partial.reshape(2, 2, 2, rows // 8, width)
    total = parts[:, :, 0].astype(F32) + swap_h(parts[:, :, 1].astype(BF16), 1).astype(F32)
    half = width // 2
    left, right = total[..., :half], total[..., half:]
    left = left[:, 0] + swap_u(left[:, 1].astype(BF16)).astype(F32)
    right = right[0] + swap_h(right[1].astype(BF16), 2).astype(F32)
    left = left[0] + swap_h(left[1].astype(BF16), 2).astype(F32)
    right = right[0] + swap_u(right[1].astype(BF16)).astype(F32)
    return jnp.concatenate([left, right], axis=-1)


def plane_reduce_small(values):
    parts = values.reshape(2, 2, 2, -1)
    total = parts[:, :, 0] + swap_h(parts[:, :, 1], 1)
    total = total[:, 0] + swap_u(total[:, 1])
    return total[0] + swap_h(total[1], 2)


def plane_gather(own):
    rows, width = own.shape
    half = width // 2
    left, right = own[:, :half], own[:, half:]
    left = jnp.stack([left, swap_h(left, 2)])
    right = jnp.stack([right, swap_u(right)])
    left = jnp.stack([left, swap_u(left)], axis=1)
    right = jnp.stack([right, swap_h(right, 2)], axis=0)
    both = jnp.concatenate([left, right], axis=-1)
    both = jnp.stack([both, swap_h(both, 1)], axis=2)
    return both.reshape(8 * rows, width)


def plane_gather_small(own):
    both = jnp.stack([own, swap_h(own, 2)])
    both = jnp.stack([both, swap_u(both)], axis=1)
    both = jnp.stack([both, swap_h(both, 1)], axis=2)
    return both


def head_gather(own):
    both = jnp.stack([own, swap_h(own, 2)])
    return jnp.stack([both, swap_h(both, 1)], axis=1)


def own_first(values, back=False):
    place = lax.axis_index("head")
    low, high = place & 1, place >> 1
    if not back:
        values = values.reshape(2, 2, values.shape[1] // 2, values.shape[2])
    values = jnp.where(high == 1, values[::-1], values)
    values = jnp.where(low == 1, values[:, ::-1], values)
    if back:
        values = values.reshape(2, 2 * values.shape[2], values.shape[3])
    return values


def from_partner(values):
    part = swap_u(values[0, 0])
    part = jnp.stack([part, swap_h(part, 1)])
    return jnp.stack([part, swap_h(part, 2)])


def pair_rows(mine, other):
    both = jnp.stack([mine, other], axis=1)
    return both.reshape(-1, both.shape[-1])


def halves(values, axis):
    size = values.shape[axis] // 2
    mine = lax.axis_index("u")
    return (
        lax.dynamic_slice_in_dim(values, mine * size, size, axis=axis),
        lax.dynamic_slice_in_dim(values, (1 - mine) * size, size, axis=axis),
    )


def in_u_order(mine, other, axis):
    first = lax.axis_index("u") == 0
    return jnp.concatenate(
        [jnp.where(first, mine, other), jnp.where(first, other, mine)], axis=axis
    )


def share_u(values, split, join):
    mine, theirs = halves(values, split)
    return in_u_order(mine, swap_u(theirs), join)


def rms_scale(values):
    return lax.rsqrt(jnp.mean(values * values, axis=-1, keepdims=True) + EPSILON)


def rms_back(values, scale, upstream):
    inner = jnp.sum(upstream * values, axis=-1, keepdims=True)
    return scale * upstream - scale * scale * scale / values.shape[-1] * values * inner


def silu_slope(values):
    sigma = jax.nn.sigmoid(values)
    return sigma * (1.0 + values * (1.0 - sigma))


def earlier_state(local_state, decay, reverse):
    count = lax.axis_size("t")
    sign = -1 if reverse else 1
    low = local_state.astype(BF16)
    if is_line():
        total = shift_t(low, sign).astype(F32)
        weight = decay
        for by in range(2, count):
            total = total + weight * shift_t(low, sign * by).astype(F32)
            weight = weight * decay
        return total
    total = shift_t(local_state, sign)
    by, weight = 1, decay
    while by < count:
        total = total + weight * shift_t(total, sign * by)
        by, weight = by * 2, weight * weight
    return total


def local(
    tokens, w_query, w_key, w_value, w_gate, w_out, w_first, w_second, w_down, decay_rate, out_grad
):
    batch, piece, width = tokens.shape
    u_index = lax.axis_index("u")
    place = lax.axis_index("head")
    count = lax.axis_size("t")
    hidden = w_first.shape[1] // PLANE
    lanes = w_query.shape[1] // PLANE
    head_dim = lanes * PLANE // decay_rate.shape[0]
    heads = lanes // head_dim
    length = piece * PLANE
    rows = batch * length

    def columns(*matrices):
        mine, theirs = zip(*(halves(m, 1) for m in matrices))
        return in_u_order(
            jnp.concatenate(mine, axis=1), swap_u(jnp.concatenate(theirs, axis=1)), 0
        )

    piece_qk = columns(w_query, w_key)
    piece_vg = columns(w_value, w_gate)
    piece_out = share_u(w_out, 0, 1)
    piece_first = share_u(w_first.T, 0, 1)
    piece_second = share_u(w_second.T, 0, 1)
    piece_down = share_u(w_down, 0, 1)
    slots_qk, end_qk = gather_t(piece_qk)
    slots_vg, end_vg = gather_t(piece_vg)
    slots_out, end_out = gather_t(after(piece_out, end_qk))
    slots_first, end_first = gather_t(after(piece_first, end_vg))
    slots_second, end_second = gather_t(after(piece_second, end_out))
    slots_down, _ = gather_t(after(piece_down, end_first))
    full_qk = jnp.concatenate(slots_qk, axis=0)
    full_vg = jnp.concatenate(slots_vg, axis=0)
    full_out = jnp.concatenate(slots_out, axis=1)
    full_first = jnp.concatenate(slots_first, axis=1)
    full_second = jnp.concatenate(slots_second, axis=1)
    full_down = jnp.concatenate(slots_down, axis=1)

    x_rows = rotate(own_first(tokens)).astype(F32)
    normed_mine = (x_rows * rms_scale(x_rows)).astype(BF16)
    normed_in = pair_rows(normed_mine, from_partner(normed_mine))
    x_own = x_rows[0, 0]
    scale_in = rms_scale(x_own)
    gy_mine = rotate(own_first(out_grad))
    gy = pair_rows(gy_mine, from_partner(gy_mine))
    gy_own = gy_mine[0, 0].astype(F32)

    rates = lax.dynamic_slice_in_dim(decay_rate, u_index * heads, heads)
    span = jnp.arange(piece // 2)
    order = jnp.arange(2)
    position = (
        (order[:, None, None] ^ u_index) * piece
        + (order[None, :, None] ^ (place & 1)) * (piece // 2)
        + span[None, None, :]
    ).reshape(length).astype(F32)
    distance = position[:, None] - position[None, :]
    causal = distance >= 0
    decay_mask = jnp.where(
        causal[None],
        jnp.exp(-rates[:, None, None] * jnp.where(causal, distance, 0.0)[None]),
        0.0,
    )
    lead = jnp.exp(-rates[None, :] * (position[:, None] + 1.0))[None, :, :, None]
    tail = jnp.exp(-rates[None, :] * (length - 1.0 - position[:, None]))[None, :, :, None]
    piece_decay = jnp.exp(-rates * length)[None, :, None, None]

    def by_head(values):
        return values.reshape(batch, length, heads, head_dim)

    def flat(values):
        return values.reshape(rows, lanes)

    def product_of(spec, left, right):
        return jnp.einsum(spec, left, right, preferred_element_type=F32)

    pre_qk = dot_nn(normed_in, full_qk)
    query_pre, key_pre = pre_qk[:, :lanes], pre_qk[:, lanes:]
    queries = by_head(jax.nn.silu(query_pre).astype(BF16))
    keys = by_head(jax.nn.silu(key_pre).astype(BF16))
    pre_vg = dot_nn(normed_in, full_vg)
    values = by_head(pre_vg[:, :lanes].astype(BF16))
    gate_lin = pre_vg[:, lanes:]
    keys_tail = (keys * tail).astype(BF16)
    queries_lead = (queries * lead).astype(BF16)
    local_state = product_of("mshd,mshe->mhde", keys_tail, values)
    state_in = earlier_state(local_state, piece_decay, False).astype(BF16)
    scores = product_of("mthd,mshd->mhts", queries, keys)
    weights = (scores * decay_mask[None]).astype(BF16)
    attn_raw = flat(
        product_of("mhts,mshd->mthd", weights, values)
        + product_of("mthd,mhde->mthe", queries_lead, state_in)
    )
    squares = plane_reduce_small(jnp.sum(attn_raw * attn_raw, axis=1))
    attn_gated = (attn_raw * gate_lin).astype(BF16)
    out_sum = plane_reduce(dot_nn(attn_gated, full_out))
    scale_own = lax.rsqrt(squares / width + EPSILON)
    resid_mid = x_own + out_sum * scale_own[:, None]
    scale_mid = rms_scale(resid_mid)
    normed_mid = plane_gather((resid_mid * scale_mid).astype(BF16))

    first_pre = dot_nt(normed_mid, full_first)
    second_pre = dot_nt(normed_mid, full_second)
    product = (first_pre * second_pre).astype(BF16)
    grad_down = scatter_t(jnp.split(dot_tn(product, gy), count, axis=1))
    dproduct = dot_nt(gy, full_down)
    dfirst = (dproduct * second_pre).astype(BF16)
    dsecond = (dproduct * first_pre).astype(BF16)
    dnormed_mid = plane_reduce(dot_nn(dfirst, full_first) + dot_nn(dsecond, full_second))
    grad_first = scatter_t(jnp.split(dot_tn(dfirst, normed_mid), count, axis=1))
    grad_second = scatter_t(jnp.split(dot_tn(dsecond, normed_mid), count, axis=1))
    down_sum = plane_reduce(dot_nn(product, full_down))
    layer_out = own_first(rotate(head_gather((resid_mid + down_sum).astype(BF16)), True), True)

    grad_mid = gy_own + rms_back(resid_mid, scale_mid, dnormed_mid)
    grad_mid_low = grad_mid.astype(BF16)
    inner = jnp.sum(grad_mid_low.astype(F32) * out_sum, axis=-1)
    coefficient = scale_own * scale_own * scale_own / width * inner
    grad_rows = plane_gather(grad_mid_low)
    scalars = plane_gather_small(jnp.stack([scale_own, coefficient], axis=-1)).reshape(rows, 2)
    attn_scale, pull = scalars[:, :1], scalars[:, 1:]
    attn_normed = attn_raw * attn_scale
    gated = (attn_normed * gate_lin).astype(BF16)
    grad_out = scatter_t(jnp.split(dot_tn(gated, grad_rows), count, axis=1))
    dgated = dot_nt(grad_rows, full_out)
    dgate = (dgated * attn_normed).astype(BF16)
    dattn = by_head((attn_scale * (dgated * gate_lin) - pull * attn_raw).astype(BF16))

    passed = product_of("mthd,mthe->mhde", queries_lead, dattn)
    state_later = earlier_state(passed, piece_decay, True).astype(BF16)
    dweights = product_of("mthe,mshe->mhts", dattn, values)
    dscores = (dweights * decay_mask[None]).astype(BF16)
    dqueries = product_of("mhts,mshd->mthd", dscores, keys) + lead * product_of(
        "mthe,mhde->mthd", dattn, state_in
    )
    dkeys = product_of("mhts,mthd->mshd", dscores, queries) + tail * product_of(
        "mshe,mhde->mshd", values, state_later
    )
    dvalues = product_of("mhts,mthe->mshe", weights, dattn) + tail * product_of(
        "mshd,mhde->mshe", keys, state_later
    )
    dquery_pre = (flat(dqueries) * silu_slope(query_pre)).astype(BF16)
    dkey_pre = (flat(dkeys) * silu_slope(key_pre)).astype(BF16)
    d_qk = jnp.concatenate([dquery_pre, dkey_pre], axis=1)
    d_vg = jnp.concatenate([flat(dvalues).astype(BF16), dgate], axis=1)
    grad_qk = scatter_t(jnp.split(dot_tn(normed_in, d_qk), count, axis=0))
    grad_vg = scatter_t(jnp.split(dot_tn(normed_in, d_vg), count, axis=0))
    dnormed_in = plane_reduce(dot_nt(d_qk, full_qk) + dot_nt(d_vg, full_vg))
    input_own = grad_mid + rms_back(x_own, scale_in, dnormed_in)
    input_grad = own_first(
        rotate(head_gather(input_own.astype(BF16)), True), True
    ).astype(F32)

    def back_columns(pair):
        mine, theirs = halves(pair, 0)
        other = swap_u(theirs.astype(BF16)).astype(F32)
        return (
            in_u_order(mine[:, :lanes], other[:, :lanes], 1),
            in_u_order(mine[:, lanes:], other[:, lanes:], 1),
        )

    def back_rows(grad):
        mine, theirs = halves(grad, 1)
        return in_u_order(mine, swap_u(theirs.astype(BF16)).astype(F32), 0)

    grad_query, grad_key = back_columns(grad_qk)
    grad_value, grad_gate = back_columns(grad_vg)
    return (
        layer_out,
        input_grad,
        grad_query,
        grad_key,
        grad_value,
        grad_gate,
        back_rows(grad_out),
        back_rows(grad_first).T,
        back_rows(grad_second).T,
        back_rows(grad_down),
    )


def solution(mesh):
    seq, head = mesh.shape["seq"], mesh.shape["head"]
    fine = Mesh(mesh.devices.reshape(seq // PLANE, PLANE, head), ("t", "u", "head"))
    seq_axes = ("t", "u")
    rows = P(None, seq_axes, None)
    inward = P(seq_axes, "head")
    outward = P("head", seq_axes)
    return jax.shard_map(
        local,
        mesh=fine,
        in_specs=(
            rows,
            inward,
            inward,
            inward,
            inward,
            outward,
            inward,
            inward,
            outward,
            P("head"),
            rows,
        ),
        out_specs=(
            rows,
            rows,
            inward,
            inward,
            inward,
            inward,
            outward,
            inward,
            inward,
            outward,
        ),
        check_vma=False,
    )
```

time: 2520 us -> 813 us (0.32)
  waiting for transfers between devices: 2130 us -> 301 us
  starting transfers between devices: 2.89 us -> 217 us
  matrix products: 194 us -> 88.8 us
  blocking collectives: 42.4 us -> 0 us
  local copies, waits for them, and re-layouts: 41.7 us -> 77.8 us
  other arithmetic: 83.1 us -> 113 us
    reduce_scatter x16 -> x0, waiting for transfers between devices: 1290 us -> none  [the longest x2 225 us: local(): lax.psum_scatter(grads[7].astype(jnp.bfloat16), 'seq', scatter_dimension=...]
    all_gather x12 -> x0, waiting for transfers between devices: 564 us -> none  [the longest x4 109 us: entering(): pieces = jax.tree.map(lambda part: lax.all_gather(part, axis), value)]
    ppermute x0 -> x136, waiting for transfers between devices: none -> 301 us  [the longest x18 124 us: gather_t(): down = lax.ppermute(down, 't', [(i + 1, i) for i in range(0, count - step)])]
    psum x5 -> x0, waiting for transfers between devices: 269 us -> none  [the longest x2 112 us: backward_pass(): lax.psum(right_contract(dfirst, w_first) + right_contract(dsecond, w_seco...]
    ppermute x0 -> x136, starting transfers between devices: none -> 217 us  [the longest x18 68.5 us: scatter_t(): up = lax.ppermute(up, 't', [(i, i + 1) for i in range(0, count - step)])]
    dot_general x72 -> x30, matrix products: 194 us -> 88.8 us  [the longest x6 32 us: dot_nn(): return jnp.dot(left, right, preferred_element_type=F32)]
  transfers between devices with their start and end apart: 33 -> 136, of which waited for: 32 -> 46; matrix products, arithmetic and copies ran while one was open for 10% -> 25% of each run, Pallas kernels for 0% -> 0%
where the time goes in v1:
time: 813 us; the launch traced here: 802 us
  waiting for transfers between devices  301 us (37%)
  starting transfers between devices  217 us (27%)
  other arithmetic  113 us (14%)
  matrix products  88.8 us (11%)
  local copies, waits for them, and re-layouts  77.8 us (10%)
    ppermute x18, waiting for transfers between devices, gather_t(): down = lax.ppermute(down, 't', [(i + 1, i) for i in range(0, count - step)])  124 us
    ppermute x18, starting transfers between devices, scatter_t(): up = lax.ppermute(up, 't', [(i, i + 1) for i in range(0, count - step)])  68.5 us
    ppermute x18, waiting for transfers between devices, scatter_t(): up = lax.ppermute(up, 't', [(i, i + 1) for i in range(0, count - step)])  60.3 us
    ppermute x28, waiting for transfers between devices, swap_u(): return lax.ppermute(value, 'u', SWAP)  56.3 us
    ppermute x30, waiting for transfers between devices, swap_h(): return lax.ppermute(value, 'head', [(i, i ^ bit) for i in range(count)])  38.1 us
    ppermute x28, starting transfers between devices, swap_u(): return lax.ppermute(value, 'u', SWAP)  34.9 us
    ppermute x18, starting transfers between devices, gather_t(): up = lax.ppermute(up, 't', [(i, i + 1) for i in range(step - 1, count - 1)])  32.1 us
    unnamed x228, local copies, waits for them, and re-layouts  32.1 us
  transfers between devices with their start and end apart: 136, of which 46 were waited for; matrix products, arithmetic and copies ran while one was open for 25% of the time, Pallas kernels for 0%

profile of v1, /device:TPU:0, one launch (start us, length us, event | category | flops | bytes accessed | tf_op | source)
XLA Modules:
  0.0 801.5 jit_solution(17484013706718172126)
XLA Ops:
  33.4 5.0 collective-permute-start.12
  43.1 5.3 collective-permute-start.5
  67.5 9.0 %collective-permute-done.15 = bf16[512,512]{1,0:T(8,128)(2,1)} collective-permute-done((bf16[512,512]{1,0:T(8,128)(2,1)}, bf16[512,512]{1,0:T(8,128)(2,1)}, u32[]{:S(2)}, u32[]{:S(2)}) %collective-permute-start.15) | collective-permute-done | bytes 524320 | tf_op jit(solution)/shard_map/ppermute | solution.py:80
  88.9 9.9 %collective-permute-done.16 = bf16[512,512]{1,0:T(8,128)(2,1)S(1)} collective-permute-done((bf16[512,512]{1,0:T(8,128)(2,1)}, bf16[512,512]{1,0:T(8,128)(2,1)S(1)}, u32[]{:S(2)}, u32[]{:S(2)}) %collective-permute-start.16) | collective-permute-done | bytes 524320 | tf_op jit(solution)/shard_map/ppermute | solution.py:80
  117.5 5.4 fusion.146
  127.0 5.5 collective-permute-start.19
  157.3 5.4 collective-permute-done.26
  180.5 8.1 %collective-permute-done.68 = bf16[128,2048]{1,0:T(8,128)(2,1)} collective-permute-done((bf16[128,2048]{1,0:T(8,128)(2,1)}, bf16[128,2048]{1,0:T(8,128)(2,1)}, u32[]{:S(2)}, u32[]{:S(2)}) %collective-permute-start.68) | collective-permute-done | bytes 524320 | tf_op jit(solution)/shard_map/ppermute | solution.py:31
  200.8 9.4 %collective-permute-done.33 = f32[2,128]{1,0:T(2,128)S(1)} collective-permute-done((f32[2,128]{1,0:T(2,128)S(1)}, f32[2,128]{1,0:T(2,128)S(1)}, u32[]{:S(2)}, u32[]{:S(2)}) %collective-permute-start.33) | collective-permute-done | bytes 1056 | tf_op jit(solution)/shard_map/ppermute | solution.py:31
  213.7 6.4 collective-permute-start.49
  229.2 5.5 collective-permute-done.45
  239.3 11.5 %collective-permute-done.70 = bf16[2,128,2048]{2,1,0:T(8,128)(2,1)S(1)} collective-permute-done((bf16[2,128,2048]{2,1,0:T(8,128)(2,1)S(1)}, bf16[2,128,2048]{2,1,0:T(8,128)(2,1)S(1)}, u32[]{:S(2)}, u32[]{:S(2)}) %collective-permute-start.70) | collective-permute-done | bytes 1048608 | tf_op jit(solution)/shard_map/ppermute | solution.py:36
  252.4 11.8 %collective-permute-done.46 = bf16[704,512]{1,0:T(8,128)(2,1)S(1)} collective-permute-done((bf16[704,512]{1,0:T(8,128)(2,1)S(1)}, bf16[704,512]{1,0:T(8,128)(2,1)S(1)}, u32[]{:S(2)}, u32[]{:S(2)}) %collective-permute-start.46) | collective-permute-done | bytes 720928 | tf_op jit(solution)/shard_map/ppermute | solution.py:80
  271.0 8.2 %collective-permute-done.56 = bf16[704,512]{1,0:T(8,128)(2,1)S(1)} collective-permute-done((bf16[704,512]{1,0:T(8,128)(2,1)S(1)}, bf16[704,512]{1,0:T(8,128)(2,1)S(1)}, u32[]{:S(2)}, u32[]{:S(2)}) %collective-permute-start.56) | collective-permute-done | bytes 720928 | tf_op jit(solution)/shard_map/ppermute | solution.py:79
  281.2 8.7 %collective-permute-done.52 = bf16[704,512]{1,0:T(8,128)(2,1)S(1)} collective-permute-done((bf16[704,512]{1,0:T(8,128)(2,1)S(1)}, bf16[704,512]{1,0:T(8,128)(2,1)S(1)}, u32[]{:S(2)}, u32[]{:S(2)}) %collective-permute-start.52) | collective-permute-done | bytes 720928 | tf_op jit(solution)/shard_map/ppermute | solution.py:80
  291.2 9.9 %collective-permute-done.55 = bf16[704,512]{1,0:T(8,128)(2,1)S(1)} collective-permute-done((bf16[704,512]{1,0:T(8,128)(2,1)S(1)}, bf16[704,512]{1,0:T(8,128)(2,1)S(1)}, u32[]{:S(2)}, u32[]{:S(2)}) %collective-permute-start.55) | collective-permute-done | bytes 720928 | tf_op jit(solution)/shard_map/ppermute | solution.py:80
  303.3 30.0 %collective-permute-done.59 = bf16[704,512]{1,0:T(8,128)(2,1)S(1)} collective-permute-done((bf16[704,512]{1,0:T(8,128)(2,1)S(1)}, bf16[704,512]{1,0:T(8,128)(2,1)S(1)}, u32[]{:S(2)}, u32[]{:S(2)}) %collective-permute-start.59) | collective-permute-done | bytes 720928 | tf_op jit(solution)/shard_map/ppermute | solution.py:80
  334.8 18.3 %collective-permute-done.60 = bf16[704,512]{1,0:T(8,128)(2,1)S(1)} collective-permute-done((bf16[704,512]{1,0:T(8,128)(2,1)S(1)}, bf16[704,512]{1,0:T(8,128)(2,1)S(1)}, u32[]{:S(2)}, u32[]{:S(2)}) %collective-permute-start.60) | collective-permute-done | bytes 720928 | tf_op jit(solution)/shard_map/ppermute | solution.py:80
  362.2 6.0 multiply_convert_fusion.4
  371.4 6.2 fusion.75
  377.5 6.1 fusion.76
  395.8 9.6 %convolution_add_fusion.1 = f32[1024,2048]{1,0:T(8,128)S(1)} fusion(f32[1024,2048]{1,0:T(8,128)} %fusion.76, bf16[1024,704]{0,1:T(8,128)(2,1)} %get-tuple-element.103, bf16[704,512]{1,0:T(8,128)(2,1)S(1)} %broadcast_select_fusion.2, bf16[704,512]{1,0:T(8,128)(2,1)S(1)} %broadcast_select_fusion.5, bf16[704,512]{1,0:T(8,128)(2,1)S(1)} %broadcast_select_fusion.8, ...), kind=kOutput, calls=%fused_computation.25 | convolution fusion | flops 2966421504 | bytes 21102592 | tf_op jit(solution)/shard_map/dot_general | solution.py:15
  415.9 7.6 collective-permute-done.122
  429.9 9.0 %collective-permute-done.115 = bf16[704,512]{1,0:T(8,128)(2,1)S(1)} collective-permute-done((bf16[704,512]{1,0:T(8,128)(2,1)S(1)}, bf16[704,512]{1,0:T(8,128)(2,1)S(1)}, u32[]{:S(2)}, u32[]{:S(2)}) %collective-permute-start.115) | collective-permute-done | bytes 720928 | tf_op jit(solution)/shard_map/ppermute | solution.py:97
  438.9 5.3 collective-permute-start.123
  445.8 8.5 %collective-permute-done.130 = bf16[704,512]{1,0:T(8,128)(2,1)S(1)} collective-permute-done((bf16[704,512]{1,0:T(8,128)(2,1)S(1)}, bf16[704,512]{1,0:T(8,128)(2,1)S(1)}, u32[]{:S(2)}, u32[]{:S(2)}) %collective-permute-start.130) | collective-permute-done | bytes 720928 | tf_op jit(solution)/shard_map/ppermute | solution.py:97
  458.2 5.0 collective-permute-start.116
  463.3 6.5 collective-permute-done.123
  475.1 5.5 collective-permute-start.131
  486.7 5.9 collective-permute-start.124
  501.4 5.6 collective-permute-start.117
  516.7 5.7 collective-permute-done.127
  536.0 5.2 collective-permute-done.135
  541.7 5.6 collective-permute-done.128
  556.7 7.7 collective-permute-done.75
  576.7 7.2 collective-permute-start.82
  588.2 10.3 %collective-permute-done.82 = bf16[2,128,1024]{2,1,0:T(8,128)(2,1)S(1)} collective-permute-done((bf16[2,128,1024]{2,1,0:T(8,128)(2,1)S(1)}, bf16[2,128,1024]{2,1,0:T(8,128)(2,1)S(1)}, u32[]{:S(2)}, u32[]{:S(2)}) %collective-permute-start.82) | collective-permute-done | bytes 524320 | tf_op jit(solution)/shard_map/ppermute | solution.py:36
  602.6 6.7 collective-permute-done.66
  650.9 5.2 collective-permute-start.108
  662.3 5.0 fusion.48
  683.5 5.8 convolution_add_fusion
  695.1 5.5 collective-permute-done.109
  711.0 10.9 %collective-permute-done.110 = bf16[256,512]{0,1:T(8,128)(2,1)S(1)} collective-permute-done((bf16[256,512]{0,1:T(8,128)(2,1)S(1)}, bf16[256,512]{0,1:T(8,128)(2,1)S(1)}, u32[]{:S(2)}, u32[]{:S(2)}) %collective-permute-start.110) | collective-permute-done | bytes 262176 | tf_op jit(solution)/shard_map/ppermute | solution.py:97
  721.9 5.2 collective-permute-start.102
  752.9 5.1 collective-permute-start.96
  761.8 5.4 collective-permute-done.106
  773.6 5.4 collective-permute-done.92
  784.7 5.2 collective-permute-done.100
  (698 shorter events, 430.3 us)
Async XLA Ops:
  3.2 45.2 %collective-permute-start.20 = (bf16[256,256]{0,1:T(8,128)(2,1)}, bf16[256,256]{0,1:T(8,128)(2,1)}, u32[]{:S(2)}, u32[]{:S(2)}) collective-permute-start(bf16[256,256]{0,1:T(8,128)(2,1)} %copy.230), channel_id=1, source_target_pairs={{0,4},{4,0},{1,5},{5,1},{2,6},{6,2},{3,7},{7,3},{8,12},{12,8},{9,1... | collective-permute-start | bytes 393224 | tf_op jit(solution)/shard_map/ppermute | solution.py:31
  10.2 29.5 %collective-permute-start.3 = (bf16[256,512]{1,0:T(8,128)(2,1)}, bf16[256,512]{1,0:T(8,128)(2,1)}, u32[]{:S(2)}, u32[]{:S(2)}) collective-permute-start(bf16[256,512]{1,0:T(8,128)(2,1)} %pad_maximum_fusion.46), channel_id=1, source_target_pairs={{0,4},{4,0},{1,5},{5,1},{2,6},{6,2},{3,7},{7,3},{8,12},{12,8},{9,1... | collective-permute-start | bytes 786440 | tf_op jit(solution)/shard_map/ppermute | solution.py:31
  19.8 36.9 %collective-permute-start = (bf16[128,2048]{1,0:T(8,128)(2,1)}, bf16[128,2048]{1,0:T(8,128)(2,1)}, u32[]{:S(2)}, u32[]{:S(2)}) collective-permute-start(bf16[128,2048]{1,0:T(8,128)(2,1)} %fusion.51), channel_id=1, source_target_pairs={{0,4},{4,0},{1,5},{5,1},{2,6},{6,2},{3,7},{7,3},{8,12},{12,8},{9,1... | collective-permute-start | bytes 1572872 | tf_op jit(solution)/shard_map/ppermute | solution.py:31
  80.8 29.5 %collective-permute-start.2 = (bf16[2,128,2048]{2,1,0:T(8,128)(2,1)S(1)}, bf16[2,128,2048]{2,1,0:T(8,128)(2,1)S(1)}, u32[]{:S(2)}, u32[]{:S(2)}) collective-permute-start(bf16[2,128,2048]{2,1,0:T(8,128)(2,1)S(1)} %get-tuple-element.164), channel_id=1, source_target_pairs={{0,2},{1,3},{2,0},{3,1},{4,6},{5,7},{6,4},{7,5},{8,10},{9,11},{10,... | collective-permute-start | bytes 3145736 | tf_op jit(solution)/shard_map/ppermute | solution.py:36
  82.4 24.1 %collective-permute-start.7 = (bf16[512,512]{1,0:T(8,128)(2,1)S(1)}, bf16[512,512]{1,0:T(8,128)(2,1)S(1)}, u32[]{:S(2)}, u32[]{:S(2)}) collective-permute-start(bf16[512,512]{1,0:T(8,128)(2,1)S(1)} %collective-permute-done.6), channel_id=1, source_target_pairs={{16,24},{17,25},{18,26},{19,27},{20,28},{21,29},{22,30},{23,31}} | collective-permute-start | bytes 1572872 | tf_op jit(solution)/shard_map/ppermute | solution.py:79
  98.9 42.1 %collective-permute-start.22 = (bf16[256,512]{0,1:T(8,128)(2,1)}, bf16[256,512]{0,1:T(8,128)(2,1)}, u32[]{:S(2)}, u32[]{:S(2)}) collective-permute-start(bf16[256,512]{0,1:T(8,128)(2,1)} %pad_maximum_fusion.49), channel_id=1, source_target_pairs={{0,8},{8,16},{16,24},{1,9},{9,17},{17,25},{2,10},{10,18},{18,26},{... | collective-permute-start | bytes 786440 | tf_op jit(solution)/shard_map/ppermute | solution.py:79
  101.1 41.6 %collective-permute-start.21 = (bf16[256,512]{0,1:T(8,128)(2,1)}, bf16[256,512]{0,1:T(8,128)(2,1)}, u32[]{:S(2)}, u32[]{:S(2)}) collective-permute-start(bf16[256,512]{0,1:T(8,128)(2,1)} %pad_maximum_fusion.49), channel_id=1, source_target_pairs={{8,0},{16,8},{24,16},{9,1},{17,9},{25,17},{10,2},{18,10},{26,18},{... | collective-permute-start | bytes 786440 | tf_op jit(solution)/shard_map/ppermute | solution.py:80
  142.7 33.3 %collective-permute-start.54 = (bf16[704,256]{1,0:T(8,128)(2,1)}, bf16[704,256]{1,0:T(8,128)(2,1)}, u32[]{:S(2)}, u32[]{:S(2)}) collective-permute-start(bf16[704,256]{1,0:T(8,128)(2,1)} %constant_dynamic-slice_fusion.4), channel_id=1, source_target_pairs={{0,4},{4,0},{1,5},{5,1},{2,6},{6,2},{3,7},{7,3},{8,12},{12,8},{9,1... | collective-permute-start | bytes 1081352 | tf_op jit(solution)/shard_map/ppermute | solution.py:31
  143.4 33.8 %collective-permute-start.40 = (bf16[704,256]{1,0:T(8,128)(2,1)}, bf16[704,256]{1,0:T(8,128)(2,1)}, u32[]{:S(2)}, u32[]{:S(2)}) collective-permute-start(bf16[704,256]{1,0:T(8,128)(2,1)} %bitcast.48), channel_id=1, source_target_pairs={{0,4},{4,0},{1,5},{5,1},{2,6},{6,2},{3,7},{7,3},{8,12},{12,8},{9,1... | collective-permute-start | bytes 1081352 | tf_op jit(solution)/shard_map/ppermute | solution.py:31
  144.8 33.5 %collective-permute-start.47 = (bf16[704,256]{1,0:T(8,128)(2,1)}, bf16[704,256]{1,0:T(8,128)(2,1)}, u32[]{:S(2)}, u32[]{:S(2)}) collective-permute-start(bf16[704,256]{1,0:T(8,128)(2,1)} %bitcast.50), channel_id=1, source_target_pairs={{0,4},{4,0},{1,5},{5,1},{2,6},{6,2},{3,7},{7,3},{8,12},{12,8},{9,1... | collective-permute-start | bytes 1081352 | tf_op jit(solution)/shard_map/ppermute | solution.py:31
  227.3 23.5 %collective-permute-start.70 = (bf16[2,128,2048]{2,1,0:T(8,128)(2,1)S(1)}, bf16[2,128,2048]{2,1,0:T(8,128)(2,1)S(1)}, u32[]{:S(2)}, u32[]{:S(2)}) collective-permute-start(bf16[2,128,2048]{2,1,0:T(8,128)(2,1)S(1)} %get-tuple-element.160), channel_id=1, source_target_pairs={{0,2},{1,3},{2,0},{3,1},{4,6},{5,7},{6,4},{7,5},{8,10},{9,11},{10,... | collective-permute-start | bytes 3145736 | tf_op jit(solution)/shard_map/ppermute | solution.py:36
  227.9 40.4 %collective-permute-start.48 = (bf16[704,512]{1,0:T(8,128)(2,1)S(1)}, bf16[704,512]{1,0:T(8,128)(2,1)S(1)}, u32[]{:S(2)}, u32[]{:S(2)}) collective-permute-start(bf16[704,512]{1,0:T(8,128)(2,1)S(1)} %pad_maximum_fusion.22), channel_id=1, source_target_pairs={{8,0},{16,8},{24,16},{9,1},{17,9},{25,17},{10,2},{18,10},{26,18},{... | collective-permute-start | bytes 2162696 | tf_op jit(solution)/shard_map/ppermute | solution.py:80
  235.4 28.7 %collective-permute-start.46 = (bf16[704,512]{1,0:T(8,128)(2,1)S(1)}, bf16[704,512]{1,0:T(8,128)(2,1)S(1)}, u32[]{:S(2)}, u32[]{:S(2)}) collective-permute-start(bf16[704,512]{1,0:T(8,128)(2,1)S(1)} %collective-permute-done.45), channel_id=1, source_target_pairs={{8,0},{9,1},{10,2},{11,3},{12,4},{13,5},{14,6},{15,7}} | collective-permute-start | bytes 2162696 | tf_op jit(solution)/shard_map/ppermute | solution.py:80
  236.7 32.9 %collective-permute-start.50 = (bf16[704,512]{1,0:T(8,128)(2,1)S(1)}, bf16[704,512]{1,0:T(8,128)(2,1)S(1)}, u32[]{:S(2)}, u32[]{:S(2)}) collective-permute-start(bf16[704,512]{1,0:T(8,128)(2,1)S(1)} %collective-permute-done.49), channel_id=1, source_target_pairs={{8,16},{16,24},{9,17},{17,25},{10,18},{18,26},{11,19},{19,27},{12,... | collective-permute-start | bytes 2162696 | tf_op jit(solution)/shard_map/ppermute | solution.py:79
  269.7 31.4 %collective-permute-start.55 = (bf16[704,512]{1,0:T(8,128)(2,1)S(1)}, bf16[704,512]{1,0:T(8,128)(2,1)S(1)}, u32[]{:S(2)}, u32[]{:S(2)}) collective-permute-start(bf16[704,512]{1,0:T(8,128)(2,1)S(1)} %copy-done.75), channel_id=1, source_target_pairs={{8,0},{16,8},{24,16},{9,1},{17,9},{25,17},{10,2},{18,10},{26,18},{... | collective-permute-start | bytes 2162696 | tf_op jit(solution)/shard_map/ppermute | solution.py:80
  279.3 23.9 %collective-permute-start.51 = (bf16[704,512]{1,0:T(8,128)(2,1)S(1)}, bf16[704,512]{1,0:T(8,128)(2,1)S(1)}, u32[]{:S(2)}, u32[]{:S(2)}) collective-permute-start(bf16[704,512]{1,0:T(8,128)(2,1)S(1)} %collective-permute-done.50), channel_id=1, source_target_pairs={{16,24},{17,25},{18,26},{19,27},{20,28},{21,29},{22,30},{23,31}} | collective-permute-start | bytes 2162696 | tf_op jit(solution)/shard_map/ppermute | solution.py:79
  281.0 72.2 %collective-permute-start.39 = (bf16[2,2,128,2048]{3,2,1,0:T(8,128)(2,1)S(1)}, bf16[2,2,128,2048]{3,2,1,0:T(8,128)(2,1)S(1)}, u32[]{:S(2)}, u32[]{:S(2)}) collective-permute-start(bf16[2,2,128,2048]{3,2,1,0:T(8,128)(2,1)S(1)} %get-tuple-element.133), channel_id=1, source_target_pairs={{0,1},{1,0},{2,3},{3,2},{4,5},{5,4},{6,7},{7,6},{8,9},{9,8},{10,11... | collective-permute-start | bytes 6291464 | tf_op jit(solution)/shard_map/ppermute | solution.py:36
  289.9 44.7 %collective-permute-start.53 = (bf16[704,512]{1,0:T(8,128)(2,1)S(1)}, bf16[704,512]{1,0:T(8,128)(2,1)S(1)}, u32[]{:S(2)}, u32[]{:S(2)}) collective-permute-start(bf16[704,512]{1,0:T(8,128)(2,1)S(1)} %collective-permute-done.52), channel_id=1, source_target_pairs={{8,0},{9,1},{10,2},{11,3},{12,4},{13,5},{14,6},{15,7}} | collective-permute-start | bytes 2162696 | tf_op jit(solution)/shard_map/ppermute | solution.py:80
  301.0 32.2 %collective-permute-start.59 = (bf16[704,512]{1,0:T(8,128)(2,1)S(1)}, bf16[704,512]{1,0:T(8,128)(2,1)S(1)}, u32[]{:S(2)}, u32[]{:S(2)}) collective-permute-start(bf16[704,512]{1,0:T(8,128)(2,1)S(1)} %collective-permute-done.55), channel_id=1, source_target_pairs={{8,0},{16,8},{9,1},{17,9},{10,2},{18,10},{11,3},{19,11},{12,4},{20... | collective-permute-start | bytes 2162696 | tf_op jit(solution)/shard_map/ppermute | solution.py:80
  302.5 32.2 %collective-permute-start.58 = (bf16[704,512]{1,0:T(8,128)(2,1)S(1)}, bf16[704,512]{1,0:T(8,128)(2,1)S(1)}, u32[]{:S(2)}, u32[]{:S(2)}) collective-permute-start(bf16[704,512]{1,0:T(8,128)(2,1)S(1)} %collective-permute-done.57), channel_id=1, source_target_pairs={{16,24},{17,25},{18,26},{19,27},{20,28},{21,29},{22,30},{23,31}} | collective-permute-start | bytes 2162696 | tf_op jit(solution)/shard_map/ppermute | solution.py:79
  388.2 24.9 %collective-permute-start.129 = (bf16[704,512]{1,0:T(8,128)(2,1)}, bf16[704,512]{1,0:T(8,128)(2,1)}, u32[]{:S(2)}, u32[]{:S(2)}) collective-permute-start(bf16[704,512]{1,0:T(8,128)(2,1)} %get-tuple-element.69), channel_id=1, source_target_pairs={{0,8},{1,9},{2,10},{3,11},{4,12},{5,13},{6,14},{7,15}} | collective-permute-start | bytes 2162696 | tf_op jit(solution)/shard_map/ppermute | solution.py:97
  407.9 31.0 %collective-permute-start.115 = (bf16[704,512]{1,0:T(8,128)(2,1)S(1)}, bf16[704,512]{1,0:T(8,128)(2,1)S(1)}, u32[]{:S(2)}, u32[]{:S(2)}) collective-permute-start(bf16[704,512]{1,0:T(8,128)(2,1)S(1)} %get-tuple-element.81), channel_id=1, source_target_pairs={{0,8},{1,9},{2,10},{3,11},{4,12},{5,13},{6,14},{7,15}} | collective-permute-start | bytes 2162696 | tf_op jit(solution)/shard_map/ppermute | solution.py:97
  413.1 82.5 %collective-permute-start.61 = (bf16[2,2,128,2048]{3,2,1,0:T(8,128)(2,1)}, bf16[2,2,128,2048]{3,2,1,0:T(8,128)(2,1)}, u32[]{:S(2)}, u32[]{:S(2)}) collective-permute-start(bf16[2,2,128,2048]{3,2,1,0:T(8,128)(2,1)} %fusion.6), channel_id=1, source_target_pairs={{0,1},{1,0},{2,3},{3,2},{4,5},{5,4},{6,7},{7,6},{8,9},{9,8},{10,11... | collective-permute-start | bytes 6291464 | tf_op jit(solution)/shard_map/ppermute | solution.py:36
  413.1 32.8 %collective-permute-start.118 = (bf16[704,512]{1,0:T(8,128)(2,1)S(1)}, bf16[704,512]{1,0:T(8,128)(2,1)S(1)}, u32[]{:S(2)}, u32[]{:S(2)}) collective-permute-start(bf16[704,512]{1,0:T(8,128)(2,1)S(1)} %get-tuple-element.82), channel_id=1, source_target_pairs={{24,16},{25,17},{26,18},{27,19},{28,20},{29,21},{30,22},{31,23}} | collective-permute-start | bytes 2162696 | tf_op jit(solution)/shard_map/ppermute | solution.py:98
  423.5 30.9 %collective-permute-start.130 = (bf16[704,512]{1,0:T(8,128)(2,1)S(1)}, bf16[704,512]{1,0:T(8,128)(2,1)S(1)}, u32[]{:S(2)}, u32[]{:S(2)}) collective-permute-start(bf16[704,512]{1,0:T(8,128)(2,1)S(1)} %get-tuple-element.67), channel_id=1, source_target_pairs={{0,8},{8,16},{1,9},{9,17},{2,10},{10,18},{3,11},{11,19},{4,12},{12... | collective-permute-start | bytes 2162696 | tf_op jit(solution)/shard_map/ppermute | solution.py:97
  427.9 29.4 %collective-permute-start.133 = (bf16[704,512]{1,0:T(8,128)(2,1)S(1)}, bf16[704,512]{1,0:T(8,128)(2,1)S(1)}, u32[]{:S(2)}, u32[]{:S(2)}) collective-permute-start(bf16[704,512]{1,0:T(8,128)(2,1)S(1)} %get-tuple-element.68), channel_id=1, source_target_pairs={{16,8},{24,16},{17,9},{25,17},{18,10},{26,18},{19,11},{27,19},{20,... | collective-permute-start | bytes 2162696 | tf_op jit(solution)/shard_map/ppermute | solution.py:98
  438.9 30.9 %collective-permute-start.123 = (bf16[704,512]{1,0:T(8,128)(2,1)S(1)}, bf16[704,512]{1,0:T(8,128)(2,1)}, u32[]{:S(2)}, u32[]{:S(2)}) collective-permute-start(bf16[704,512]{1,0:T(8,128)(2,1)S(1)} %get-tuple-element.73), channel_id=1, source_target_pairs={{0,8},{8,16},{1,9},{9,17},{2,10},{10,18},{3,11},{11,19},{4,12},{12... | collective-permute-start | bytes 2162696 | tf_op jit(solution)/shard_map/ppermute | solution.py:97
  445.8 55.6 %collective-permute-start.71 = (bf16[2,2,128,2048]{3,2,1,0:T(8,128)(2,1)}, bf16[2,2,128,2048]{3,2,1,0:T(8,128)(2,1)}, u32[]{:S(2)}, u32[]{:S(2)}) collective-permute-start(bf16[2,2,128,2048]{3,2,1,0:T(8,128)(2,1)} %fusion.7), channel_id=1, source_target_pairs={{0,1},{1,0},{2,3},{3,2},{4,5},{5,4},{6,7},{7,6},{8,9},{9,8},{10,11... | collective-permute-start | bytes 6291464 | tf_op jit(solution)/shard_map/ppermute | solution.py:36
  458.2 27.1 %collective-permute-start.116 = (bf16[704,512]{1,0:T(8,128)(2,1)}, bf16[704,512]{1,0:T(8,128)(2,1)}, u32[]{:S(2)}, u32[]{:S(2)}) collective-permute-start(bf16[704,512]{1,0:T(8,128)(2,1)} %get-tuple-element.79), channel_id=1, source_target_pairs={{0,8},{8,16},{1,9},{9,17},{2,10},{10,18},{3,11},{11,19},{4,12},{12... | collective-permute-start | bytes 2162696 | tf_op jit(solution)/shard_map/ppermute | solution.py:97
  475.1 34.7 %collective-permute-start.131 = (bf16[704,512]{1,0:T(8,128)(2,1)}, bf16[704,512]{1,0:T(8,128)(2,1)}, u32[]{:S(2)}, u32[]{:S(2)}) collective-permute-start(bf16[704,512]{1,0:T(8,128)(2,1)} %get-tuple-element.65), channel_id=1, source_target_pairs={{0,8},{8,16},{16,24},{1,9},{9,17},{17,25},{2,10},{10,18},{18,26},{... | collective-permute-start | bytes 2162696 | tf_op jit(solution)/shard_map/ppermute | solution.py:97
  485.4 25.9 %collective-permute-start.134 = (bf16[704,512]{1,0:T(8,128)(2,1)S(1)}, bf16[704,512]{1,0:T(8,128)(2,1)}, u32[]{:S(2)}, u32[]{:S(2)}) collective-permute-start(bf16[704,512]{1,0:T(8,128)(2,1)S(1)} %get-tuple-element.66), channel_id=1, source_target_pairs={{8,0},{16,8},{24,16},{9,1},{17,9},{25,17},{10,2},{18,10},{26,18},{... | collective-permute-start | bytes 2162696 | tf_op jit(solution)/shard_map/ppermute | solution.py:98
  486.7 29.5 %collective-permute-start.124 = (bf16[704,512]{1,0:T(8,128)(2,1)S(1)}, bf16[704,512]{1,0:T(8,128)(2,1)}, u32[]{:S(2)}, u32[]{:S(2)}) collective-permute-start(bf16[704,512]{1,0:T(8,128)(2,1)S(1)} %get-tuple-element.71), channel_id=1, source_target_pairs={{0,8},{8,16},{16,24},{1,9},{9,17},{17,25},{2,10},{10,18},{18,26},{... | collective-permute-start | bytes 2162696 | tf_op jit(solution)/shard_map/ppermute | solution.py:97
  495.6 26.8 %collective-permute-start.127 = (bf16[704,512]{1,0:T(8,128)(2,1)S(1)}, bf16[704,512]{1,0:T(8,128)(2,1)}, u32[]{:S(2)}, u32[]{:S(2)}) collective-permute-start(bf16[704,512]{1,0:T(8,128)(2,1)S(1)} %get-tuple-element.72), channel_id=1, source_target_pairs={{8,0},{16,8},{24,16},{9,1},{17,9},{25,17},{10,2},{18,10},{26,18},{... | collective-permute-start | bytes 2162696 | tf_op jit(solution)/shard_map/ppermute | solution.py:98
  501.4 28.4 %collective-permute-start.117 = (bf16[704,512]{1,0:T(8,128)(2,1)}, bf16[704,512]{1,0:T(8,128)(2,1)}, u32[]{:S(2)}, u32[]{:S(2)}) collective-permute-start(bf16[704,512]{1,0:T(8,128)(2,1)} %get-tuple-element.77), channel_id=1, source_target_pairs={{0,8},{8,16},{16,24},{1,9},{9,17},{17,25},{2,10},{10,18},{18,26},{... | collective-permute-start | bytes 2162696 | tf_op jit(solution)/shard_map/ppermute | solution.py:97
  509.8 23.5 %collective-permute-start.120 = (bf16[704,512]{1,0:T(8,128)(2,1)S(1)}, bf16[704,512]{1,0:T(8,128)(2,1)S(1)}, u32[]{:S(2)}, u32[]{:S(2)}) collective-permute-start(bf16[704,512]{1,0:T(8,128)(2,1)S(1)} %get-tuple-element.78), channel_id=1, source_target_pairs={{8,0},{16,8},{24,16},{9,1},{17,9},{25,17},{10,2},{18,10},{26,18},{... | collective-permute-start | bytes 2162696 | tf_op jit(solution)/shard_map/ppermute | solution.py:98
  511.2 37.6 %collective-permute-start.62 = (bf16[2,128,1024]{2,1,0:T(8,128)(2,1)S(1)}, bf16[2,128,1024]{2,1,0:T(8,128)(2,1)S(1)}, u32[]{:S(2)}, u32[]{:S(2)}) collective-permute-start(bf16[2,128,1024]{2,1,0:T(8,128)(2,1)S(1)} %slice_bitcast_fusion.19), channel_id=1, source_target_pairs={{0,4},{4,0},{1,5},{5,1},{2,6},{6,2},{3,7},{7,3},{8,12},{12,8},{9,1... | collective-permute-start | bytes 1572872 | tf_op jit(solution)/shard_map/ppermute | solution.py:31
  516.2 32.7 %collective-permute-start.64 = (bf16[2,128,1024]{2,1,0:T(8,128)(2,1)S(1)}, bf16[2,128,1024]{2,1,0:T(8,128)(2,1)S(1)}, u32[]{:S(2)}, u32[]{:S(2)}) collective-permute-start(bf16[2,128,1024]{2,1,0:T(8,128)(2,1)S(1)} %copy-done.82), channel_id=1, source_target_pairs={{0,2},{1,3},{2,0},{3,1},{4,6},{5,7},{6,4},{7,5},{8,10},{9,11},{10,... | collective-permute-start | bytes 1572872 | tf_op jit(solution)/shard_map/ppermute | solution.py:36
  522.3 26.9 %collective-permute-start.72 = (bf16[2,128,1024]{2,1,0:T(8,128)(2,1)S(1)}, bf16[2,128,1024]{2,1,0:T(8,128)(2,1)S(1)}, u32[]{:S(2)}, u32[]{:S(2)}) collective-permute-start(bf16[2,128,1024]{2,1,0:T(8,128)(2,1)S(1)} %slice_bitcast_fusion.15), channel_id=1, source_target_pairs={{0,4},{4,0},{1,5},{5,1},{2,6},{6,2},{3,7},{7,3},{8,12},{12,8},{9,1... | collective-permute-start | bytes 1572872 | tf_op jit(solution)/shard_map/ppermute | solution.py:31
  547.4 64.9 %collective-permute-start.121 = (bf16[704,256]{1,0:T(8,128)(2,1)S(1)}, bf16[704,256]{1,0:T(8,128)(2,1)S(1)}, u32[]{:S(2)}, u32[]{:S(2)}) collective-permute-start(bf16[704,256]{1,0:T(8,128)(2,1)S(1)} %dynamic-slice_convert_fusion.2), channel_id=1, source_target_pairs={{0,4},{4,0},{1,5},{5,1},{2,6},{6,2},{3,7},{7,3},{8,12},{12,8},{9,1... | collective-permute-start | bytes 1081352 | tf_op jit(solution)/shard_map/ppermute | solution.py:31
  586.1 24.7 %collective-permute-start.76 = (f32[128,2]{0,1:T(2,128)S(1)}, f32[128,2]{0,1:T(2,128)S(1)}, u32[]{:S(2)}, u32[]{:S(2)}) collective-permute-start(f32[128,2]{0,1:T(2,128)S(1)} %get-tuple-element.216), channel_id=1, source_target_pairs={{0,2},{1,3},{2,0},{3,1},{4,6},{5,7},{6,4},{7,5},{8,10},{9,11},{10,... | collective-permute-start | bytes 3080 | tf_op jit(solution)/shard_map/ppermute | solution.py:36
  650.9 40.4 %collective-permute-start.108 = (bf16[256,512]{0,1:T(8,128)(2,1)}, bf16[256,512]{0,1:T(8,128)(2,1)}, u32[]{:S(2)}, u32[]{:S(2)}) collective-permute-start(bf16[256,512]{0,1:T(8,128)(2,1)} %get-tuple-element.112), channel_id=1, source_target_pairs={{0,8},{1,9},{2,10},{3,11},{4,12},{5,13},{6,14},{7,15}} | collective-permute-start | bytes 786440 | tf_op jit(solution)/shard_map/ppermute | solution.py:97
  656.1 35.2 %collective-permute-start.111 = (bf16[256,512]{0,1:T(8,128)(2,1)}, bf16[256,512]{0,1:T(8,128)(2,1)}, u32[]{:S(2)}, u32[]{:S(2)}) collective-permute-start(bf16[256,512]{0,1:T(8,128)(2,1)} %get-tuple-element.113), channel_id=1, source_target_pairs={{24,16},{25,17},{26,18},{27,19},{28,20},{29,21},{30,22},{31,23}} | collective-permute-start | bytes 786440 | tf_op jit(solution)/shard_map/ppermute | solution.py:98
  672.4 33.5 %collective-permute-start.101 = (bf16[512,512]{0,1:T(8,128)(2,1)}, bf16[512,512]{0,1:T(8,128)(2,1)}, u32[]{:S(2)}, u32[]{:S(2)}) collective-permute-start(bf16[512,512]{0,1:T(8,128)(2,1)} %get-tuple-element.87), channel_id=1, source_target_pairs={{0,8},{1,9},{2,10},{3,11},{4,12},{5,13},{6,14},{7,15}} | collective-permute-start | bytes 1572872 | tf_op jit(solution)/shard_map/ppermute | solution.py:97
  677.3 29.9 %collective-permute-start.104 = (bf16[512,512]{0,1:T(8,128)(2,1)}, bf16[512,512]{0,1:T(8,128)(2,1)}, u32[]{:S(2)}, u32[]{:S(2)}) collective-permute-start(bf16[512,512]{0,1:T(8,128)(2,1)} %get-tuple-element.88), channel_id=1, source_target_pairs={{24,16},{25,17},{26,18},{27,19},{28,20},{29,21},{30,22},{31,23}} | collective-permute-start | bytes 1572872 | tf_op jit(solution)/shard_map/ppermute | solution.py:98
  691.3 45.0 %collective-permute-start.87 = (bf16[2,2,128,2048]{3,2,1,0:T(8,128)(2,1)}, bf16[2,2,128,2048]{3,2,1,0:T(8,128)(2,1)}, u32[]{:S(2)}, u32[]{:S(2)}) collective-permute-start(bf16[2,2,128,2048]{3,2,1,0:T(8,128)(2,1)} %fusion.8), channel_id=1, source_target_pairs={{0,1},{1,0},{2,3},{3,2},{4,5},{5,4},{6,7},{7,6},{8,9},{9,8},{10,11... | collective-permute-start | bytes 6291464 | tf_op jit(solution)/shard_map/ppermute | solution.py:36
  700.6 28.0 %collective-permute-start.94 = (bf16[512,512]{0,1:T(8,128)(2,1)S(1)}, bf16[512,512]{0,1:T(8,128)(2,1)S(1)}, u32[]{:S(2)}, u32[]{:S(2)}) collective-permute-start(bf16[512,512]{0,1:T(8,128)(2,1)S(1)} %get-tuple-element.93), channel_id=1, source_target_pairs={{0,8},{1,9},{2,10},{3,11},{4,12},{5,13},{6,14},{7,15}} | collective-permute-start | bytes 1572872 | tf_op jit(solution)/shard_map/ppermute | solution.py:97
  705.0 25.2 %collective-permute-start.97 = (bf16[512,512]{0,1:T(8,128)(2,1)S(1)}, bf16[512,512]{0,1:T(8,128)(2,1)S(1)}, u32[]{:S(2)}, u32[]{:S(2)}) collective-permute-start(bf16[512,512]{0,1:T(8,128)(2,1)S(1)} %get-tuple-element.94), channel_id=1, source_target_pairs={{24,16},{25,17},{26,18},{27,19},{28,20},{29,21},{30,22},{31,23}} | collective-permute-start | bytes 1572872 | tf_op jit(solution)/shard_map/ppermute | solution.py:98
  752.9 27.2 %collective-permute-start.96 = (bf16[512,512]{0,1:T(8,128)(2,1)S(1)}, bf16[512,512]{0,1:T(8,128)(2,1)S(1)}, u32[]{:S(2)}, u32[]{:S(2)}) collective-permute-start(bf16[512,512]{0,1:T(8,128)(2,1)S(1)} %get-tuple-element.89), channel_id=1, source_target_pairs={{0,8},{8,16},{16,24},{1,9},{9,17},{17,25},{2,10},{10,18},{18,26},{... | collective-permute-start | bytes 1572872 | tf_op jit(solution)/shard_map/ppermute | solution.py:97
  (194 other events, 3090.3 us)
